TPU v7x, 128 devices: a whole 4x4x4 slice. The times are simulated.
128 devices in a mesh: win: 4 (over y_lo, core), srow: 4 (over x), scol: 8 (over z, y_hi).
Axes of the slice: x: 4, y: 4 (y_hi: 2, y_lo: 2; y = y_hi * 2 + y_lo), z: 4, core: 2. Of those that a mesh axis runs over, the one named last changes fastest.
Arguments:
- spectra: float32 [4, 2, 64, 4096], P(None, None, 'win', ('srow', 'scol')), may hold values from -6 to 6
- bins: int32 [4], replicated, may hold values from 1 to 2047
- travel: int32 [4096, 2048], P(('srow', 'scol'), 'win'), may hold values from 0 to 16383
Outputs:
- coherence: bfloat16 [4, 2, 4096, 4, 1024], P('win', None, 'srow', None, 'scol')
- beam: float32 [4, 2048], P('win')
All inputs are finite; a program needn't handle non-finite values.
Results may differ from a plain program's by a relative error of at most 0.012.
Values may be sent and summed in bfloat16 or wider, within the bound.
No kernel may reach another device: no remote copies, remote signals or barrier semaphores. Data moves between devices by JAX's collectives and lax.ppermute only.
A program may use at most 128 MiB of HBM per device.

v0:
```python
import jax
import jax.numpy as jnp
from jax import lax
from jax.experimental import pallas as pl
from jax.experimental.pallas import tpu as pltpu
from jax.sharding import PartitionSpec as P


S = 4096
NFFT = 4096
F = 4
NST = 128
NPT = 512
ALL = ("win", "srow", "scol")
ROW_OFF = (0, 1, 2, -3, 4)
ROW_WEIGHT = (1.0, 2.0, 2.0, 2.0, 1.0)
RELAY = (4, 6, 7)
ROUND = 12582912.0
STEP = 128

ROOT2 = 2.0**0.5
SIN = [ROOT2 * v for v in (3.141592580044453, -5.167706878911761, 2.5500313770692338,
                           -0.5980451729935192, 0.07722012694435497)]
COS = [-ROOT2 * v for v in (0.9999999534664096, -4.93479285864205, 4.058411913501759,
                            -1.331880156986464, 0.2196967900729894)]


def prep_kernel(spectra, travel, payload):
    for f in range(F):
        re = spectra[f, 0]
        im = spectra[f, 1]
        magnitude = jnp.sqrt(re * re + im * im + 0.5)
        for c, part in enumerate((re, im)):
            value = (part / magnitude).astype(jnp.bfloat16).astype(jnp.float32) * 32768.0
            value = jnp.clip((value + ROUND) - ROUND, -32767.0, 32767.0)
            at = NPT + 32 * f + 16 * c
            payload[at:at + 16, :] = value.astype(jnp.int32).astype(jnp.int16)
    payload[0:NPT, :] = travel[...].T.astype(jnp.int16)


def steer_kernel(bins, *refs):
    payloads, out = refs[:-1], refs[-1]
    rows = 64
    for n, ref in enumerate(payloads):
        def chunk(i, carry, n=n, ref=ref):
            at = pl.ds(pl.multiple_of(i * rows, rows), rows)
            samples = (ref[at, :].astype(jnp.int32) & (NFFT - 1)).astype(jnp.float32)
            for f in range(F):
                scale = bins[f].astype(jnp.float32) * (1.0 / NFFT)
                turns = samples * scale
                r = turns - ((turns + ROUND) - ROUND)
                z = r * r
                s = SIN[4]
                c = COS[4]
                for k in (3, 2, 1, 0):
                    s = s * z + SIN[k]
                    c = c * z + COS[k]
                s = s * r
                out[f, 0, n, at, :] = (1.0 - s * s).astype(jnp.bfloat16)
                out[f, 1, n, at, :] = (s * c).astype(jnp.bfloat16)
            return carry

        lax.fori_loop(0, STEP // rows, chunk, 0)


def steer(bins, payloads):
    n = len(payloads)
    return pl.pallas_call(
        steer_kernel,
        grid=(NPT // STEP,),
        out_shape=jax.ShapeDtypeStruct((F, 2, n, NPT, NST), jnp.bfloat16),
        in_specs=[pl.BlockSpec(memory_space=pltpu.SMEM)]
        + [pl.BlockSpec((STEP, NST), lambda i: (i, 0))] * n,
        out_specs=pl.BlockSpec((F, 2, n, STEP, NST), lambda i: (0, 0, 0, i, 0)),
    )(bins, *payloads)


def decode(sources, block):
    return [
        (a[block].astype(jnp.int32).astype(jnp.float32) * (1.0 / 32768.0)).astype(jnp.bfloat16)
        for a in sources
    ]


def beam_kernel(own_steer, col_steer, row_steer, a0, a1, a2, a3, beam, cols, weights):
    sources = (a0, a1, a2, a3)
    for d in range(4):
        cols[d * NST:(d + 1) * NST, :] = jnp.concatenate(decode(sources, d), axis=0).T

    def coherent(k):
        parts = decode(sources, 0 if k == 0 else 3 + k)
        x = jnp.concatenate(parts, axis=0)
        z = jnp.concatenate([q for v in parts for q in (v[16:32], -v[0:16])], axis=0)
        right = jnp.concatenate([x, z], axis=1)
        for j in range(4):
            at = slice(j * NST, (j + 1) * NST)
            cross = jnp.dot(cols[at, :], right, preferred_element_type=jnp.float32)
            re = cross[:, :NST]
            im = cross[:, NST:]
            inverse = lax.rsqrt(re * re + im * im + 64.0)
            if ROW_WEIGHT[k] != 1.0:
                inverse = inverse * ROW_WEIGHT[k]
            re = (re * inverse).astype(jnp.bfloat16)
            im = (im * inverse).astype(jnp.bfloat16)
            weights[k, at, :NST] = re
            weights[k, at, NST:] = im
            at = slice((4 + j) * NST, (5 + j) * NST)
            weights[k, at, :NST] = -im
            weights[k, at, NST:] = re

    steer_cols = jnp.concatenate(
        [ref for part in range(2) for ref in (own_steer[0, part, 0], *(row_steer[0, part, n] for n in range(3)))],
        axis=1,
    )
    total = None
    coherent(0)
    for k in range(5):
        if k < 4:
            coherent(k + 1)
        image = jnp.dot(steer_cols, weights[k], preferred_element_type=jnp.float32)
        re, im = (own_steer[0, 0, 0], own_steer[0, 1, 0]) if k == 0 else (col_steer[0, 0, k - 1], col_steer[0, 1, k - 1])
        power = re.astype(jnp.float32) * image[:, :NST] + im.astype(jnp.float32) * image[:, NST:]
        total = power if total is None else total + power
    for j in range(4):
        value = jnp.sum(total[j * NST:(j + 1) * NST, :].T, axis=0, keepdims=True) * (1.0 / S)
        beam[0, :, j, :] = jnp.broadcast_to(value, (32, NST))


def beams(own_steer, col_steer, row_steer, spectra):
    piece = pl.BlockSpec((8, 32, NST), lambda f: (0, f, 0))
    phases = lambda n: pl.BlockSpec((1, 2, n, NPT, NST), lambda f: (f, 0, 0, 0, 0))
    return pl.pallas_call(
        beam_kernel,
        grid=(F,),
        out_shape=jax.ShapeDtypeStruct((F, 32, 4, NST), jnp.float32),
        in_specs=[phases(1), phases(4), phases(3), piece, piece, piece, piece],
        out_specs=pl.BlockSpec((1, 32, 4, NST), lambda f: (f, 0, 0, 0)),
        scratch_shapes=[
            pltpu.VMEM((4 * NST, NST), jnp.bfloat16),
            pltpu.VMEM((5, 8 * NST, 2 * NST), jnp.bfloat16),
        ],
        name="beams",
    )(own_steer, col_steer, row_steer, *spectra)


def pack_kernel(place, a0, a1, a2, a3, rows):
    for s, a in enumerate((a0, a1, a2, a3)):
        for n, block in enumerate(RELAY):
            rows[s, n] = a[block]


def pack(place, spectra):
    own = pl.BlockSpec((8, 32, NST), lambda n, place: (0, place[0], 0))
    return pl.pallas_call(
        pack_kernel,
        grid_spec=pltpu.PrefetchScalarGridSpec(
            num_scalar_prefetch=1,
            grid=(1,),
            in_specs=[own] * 4,
            out_specs=pl.BlockSpec((4, 3, 32, NST), lambda n, place: (0, 0, 0, 0)),
        ),
        out_shape=jax.ShapeDtypeStruct((4, 3, 32, NST), jnp.int16),
        name="pack",
    )(place, *spectra)


def tile_kernel(place, rows, a0, a1, a2, a3, coherence, cols, scratch):
    n = pl.program_id(0)
    sources = (a0, a1, a2, a3)

    @pl.when(n == 0)
    def _():
        for d in range(4):
            parts = decode(sources, d)
            x = jnp.concatenate(parts, axis=0)
            y = jnp.concatenate([q for v in parts for q in (-v[16:32], v[0:16])], axis=0)
            cols[d] = jnp.concatenate([x, y], axis=1)

    def emit(parts):
        left = jnp.concatenate(parts, axis=0).T
        for d in range(4):
            cross = jnp.dot(left, cols[d], preferred_element_type=jnp.float32)
            re = cross[:, :NST]
            im = cross[:, NST:]
            inverse = lax.rsqrt(re * re + im * im + 64.0)
            at = pl.ds((place[1] + d) & 3, NST, stride=4)
            scratch[0, at, :] = re * inverse
            scratch[1, at, :] = im * inverse
        coherence[0] = scratch[0].astype(jnp.bfloat16)
        coherence[1] = scratch[1].astype(jnp.bfloat16)

    @pl.when(n < 5)
    def _():
        emit(decode(sources, jnp.where(n == 0, 0, n + 3)))

    @pl.when(n >= 5)
    def _():
        emit(decode([rows.at[k] for k in range(4)], n - 5))


def tile(place, rows, spectra):
    own = pl.BlockSpec((8, 32, NST), lambda n, place: (0, place[0], 0))

    def at(n, place):
        far = jnp.where(n == 3, -3, jnp.where(n < 5, n, jnp.where(n == 5, 3, 5 - n)))
        return (0, (place[2] + far) & 7, 0)

    return pl.pallas_call(
        tile_kernel,
        grid_spec=pltpu.PrefetchScalarGridSpec(
            num_scalar_prefetch=1,
            grid=(8,),
            in_specs=[pl.BlockSpec((4, 3, 32, NST), lambda n, place: (0, 0, 0, 0)), own, own, own, own],
            out_specs=pl.BlockSpec((2, 4 * NST, NST), at),
            scratch_shapes=[
                pltpu.VMEM((4, NST, 2 * NST), jnp.bfloat16),
                pltpu.VMEM((2, 4 * NST, NST), jnp.float32),
            ],
        ),
        out_shape=jax.ShapeDtypeStruct((2, 4 * 1024, NST), jnp.bfloat16),
        name="tile",
    )(place, rows, *spectra)


def from_offset(value, axis, offset):
    size = lax.axis_size(axis)
    return lax.ppermute(value, axis, [((i + offset) % size, i) for i in range(size)])


def from_partner(value, bit):
    return lax.ppermute(value, "win", [(i ^ bit, i) for i in range(4)])


def local(spectra, bins, travel):
    payload = pl.pallas_call(
        prep_kernel,
        out_shape=jax.ShapeDtypeStruct((NPT + 32 * F, NST), jnp.int16),
        name="prep",
    )(spectra, travel)
    place = jnp.stack([lax.axis_index(a) for a in ALL]).astype(jnp.int32)
    by_row = [from_offset(payload, "srow", d) for d in (1, 2, 3)]
    by_col = [from_offset(payload, "scol", d) for d in ROW_OFF[1:]]
    steer0 = steer(bins, [payload])
    steer2 = steer(bins, by_row)
    by_col, steer0, steer2 = lax.optimization_barrier((by_col, steer0, steer2))
    a0 = jnp.stack([v[NPT:] for v in [payload] + by_row + by_col])
    a1 = from_partner(a0, 2)
    a2 = from_partner(a0, 1)
    steer1 = steer(bins, by_col)
    a1, steer1 = lax.optimization_barrier((a1, steer1))
    a3 = from_partner(a1, 1)
    sources = (a0, a1, a2, a3)
    packed = pack(place, sources)
    rows = from_offset(packed, "scol", 2)
    partial = beams(steer0, steer1, steer2, sources)
    shares = lax.all_to_all(partial.reshape(128, 4, NST), ALL, 0, 0, tiled=True)
    coherence = tile(place, rows, sources)
    beam = shares.reshape(4, 32, 4, NST).sum(axis=1).reshape(1, 4 * NPT)
    return coherence.reshape(1, 2, 1024, 4, NST), beam


def solution(mesh):
    placed = (P(None, None, "win", ("srow", "scol")), P(), P(("srow", "scol"), "win"))
    return jax.shard_map(
        local,
        mesh=mesh,
        in_specs=placed,
        out_specs=(P("win", None, "srow", None, "scol"), P("win", None)),
        check_vma=False,
    )
```

profile of v0, /device:TPU:0, one launch (start us, length us, event | category | flops | bytes accessed | tf_op | source)
XLA Modules:
  0.0 78.6 jit_solution(14178027654211752105)
XLA Ops:
  0.6 1.8 %prep.1.refs_0_ = s16[640,128]{1,0:T(8,128)(2,1)} custom-call(f32[4,2,16,128]{3,2,1,0:T(8,128)} %spectra.1, s32[128,512]{1,0:T(8,128)} %travel.1), custom_call_target="tpu_custom_call" | custom-call | tf_op jit(solution)/shard_map/prep/pallas_call | solution.py:235
  2.4 1.6 %collective-permute-start.2 = (s16[640,128]{1,0:T(8,128)(2,1)}, s16[640,128]{1,0:T(8,128)(2,1)S(1)}, u32[]{:S(2)}, u32[]{:S(2)}) collective-permute-start(s16[640,128]{1,0:T(8,128)(2,1)} %prep.1.refs_0_), channel_id=1, source_target_pairs={{24,0},{0,8},{8,16},{16,24},{25,1},{1,9},{9,17},{17,25},{26,2},{2,... | collective-permute-start | bytes 491528 | tf_op jit(solution)/shard_map/ppermute | solution.py:227
  4.0 2.7 %collective-permute-start.1 = (s16[640,128]{1,0:T(8,128)(2,1)}, s16[640,128]{1,0:T(8,128)(2,1)S(1)}, u32[]{:S(2)}, u32[]{:S(2)}) collective-permute-start(s16[640,128]{1,0:T(8,128)(2,1)} %prep.1.refs_0_), channel_id=1, source_target_pairs={{16,0},{24,8},{0,16},{8,24},{17,1},{25,9},{1,17},{9,25},{18,2},{26... | collective-permute-start | bytes 491528 | tf_op jit(solution)/shard_map/ppermute | solution.py:227
  6.8 3.9 %collective-permute-start.6 = (s16[640,128]{1,0:T(8,128)(2,1)}, s16[640,128]{1,0:T(8,128)(2,1)S(1)}, u32[]{:S(2)}, u32[]{:S(2)}) collective-permute-start(s16[640,128]{1,0:T(8,128)(2,1)} %prep.1.refs_0_), channel_id=1, source_target_pairs={{4,0},{5,1},{6,2},{7,3},{0,4},{1,5},{2,6},{3,7},{12,8},{13,9},{14,... | collective-permute-start | bytes 491528 | tf_op jit(solution)/shard_map/ppermute | solution.py:227
  10.6 3.6 %collective-permute-start.5 = (s16[640,128]{1,0:T(8,128)(2,1)}, s16[640,128]{1,0:T(8,128)(2,1)S(1)}, u32[]{:S(2)}, u32[]{:S(2)}) collective-permute-start(s16[640,128]{1,0:T(8,128)(2,1)} %prep.1.refs_0_), channel_id=1, source_target_pairs={{5,0},{6,1},{7,2},{0,3},{1,4},{2,5},{3,6},{4,7},{13,8},{14,9},{15,... | collective-permute-start | bytes 491528 | tf_op jit(solution)/shard_map/ppermute | solution.py:227
  14.3 2.2 %collective-permute-start.4 = (s16[640,128]{1,0:T(8,128)(2,1)}, s16[640,128]{1,0:T(8,128)(2,1)S(1)}, u32[]{:S(2)}, u32[]{:S(2)}) collective-permute-start(s16[640,128]{1,0:T(8,128)(2,1)} %prep.1.refs_0_), channel_id=1, source_target_pairs={{2,0},{3,1},{4,2},{5,3},{6,4},{7,5},{0,6},{1,7},{10,8},{11,9},{12,... | collective-permute-start | bytes 491528 | tf_op jit(solution)/shard_map/ppermute | solution.py:227
  16.5 3.5 %shard_map.50.own_steer = bf16[4,2,1,512,128]{4,3,2,1,0:T(8,128)(2,1)} custom-call(s32[4]{0:T(128)} %bins.5, s16[640,128]{1,0:T(8,128)(2,1)} %prep.1.refs_0_), custom_call_target="tpu_custom_call" | custom-call | tf_op jit(solution)/shard_map/pallas_call | solution.py:68
  20.6 1.4 %collective-permute-start = (s16[640,128]{1,0:T(8,128)(2,1)}, s16[640,128]{1,0:T(8,128)(2,1)S(1)}, u32[]{:S(2)}, u32[]{:S(2)}) collective-permute-start(s16[640,128]{1,0:T(8,128)(2,1)} %prep.1.refs_0_), channel_id=1, source_target_pairs={{8,0},{16,8},{24,16},{0,24},{9,1},{17,9},{25,17},{1,25},{10,2},{18... | collective-permute-start | bytes 491528 | tf_op jit(solution)/shard_map/ppermute | solution.py:227
  22.0 0.8 %fusion.3 = s16[8,128,128]{2,1,0:T(8,128)(2,1)S(1)} fusion(s16[640,128]{1,0:T(8,128)(2,1)} %prep.1.refs_0_), kind=kLoop, calls=%fused_computation.8 | loop fusion | bytes 65536
  22.8 3.3 %collective-permute-done.refs_0_ = s16[640,128]{1,0:T(8,128)(2,1)S(1)} collective-permute-done((s16[640,128]{1,0:T(8,128)(2,1)}, s16[640,128]{1,0:T(8,128)(2,1)S(1)}, u32[]{:S(2)}, u32[]{:S(2)}) %collective-permute-start) | collective-permute-done | bytes 163872 | tf_op jit(solution)/shard_map/ppermute | solution.py:227
  26.8 5.0 %shard_map.51.row_steer = bf16[4,2,3,512,128]{4,3,2,1,0:T(8,128)(2,1)} custom-call(s32[4]{0:T(128)} %bins.5, s16[640,128]{1,0:T(8,128)(2,1)} %copy-done.10, s16[640,128]{1,0:T(8,128)(2,1)} %copy-done.9, s16[640,128]{1,0:T(8,128)(2,1)} %copy-done.8), custom_call_target="tpu_custom_call" | custom-call | tf_op jit(solution)/shard_map/pallas_call | solution.py:68
  31.9 0.8 %fusion.2 = s16[8,128,128]{2,1,0:T(8,128)(2,1)S(1)} fusion(s16[8,128,128]{2,1,0:T(8,128)(2,1)S(1)} %fusion.3, s16[640,128]{1,0:T(8,128)(2,1)} %copy-done.10), kind=kLoop, calls=%fused_computation.6 | loop fusion | bytes 65536
  32.7 0.8 fusion.1
  33.5 0.8 fusion
  34.3 1.7 %collective-permute-start.7 = (s16[8,128,128]{2,1,0:T(8,128)(2,1)S(1)}, s16[8,128,128]{2,1,0:T(8,128)(2,1)S(1)}, u32[]{:S(2)}, u32[]{:S(2)}) collective-permute-start(s16[8,128,128]{2,1,0:T(8,128)(2,1)S(1)} %bitcast_dynamic-update-slice_fusion.a0), channel_id=1, source_target_pairs={{64,0},{96,32},{0,64},{32,96},{65,1},{97,33},{1,65},{33,97},{66,2}... | collective-permute-start | bytes 786440 | tf_op jit(solution)/shard_map/ppermute | solution.py:231
  36.0 5.9 %shard_map.52.col_steer = bf16[4,2,4,512,128]{4,3,2,1,0:T(8,128)(2,1)} custom-call(s32[4]{0:T(128)} %bins.5, s16[640,128]{1,0:T(8,128)(2,1)} %copy-done.7, s16[640,128]{1,0:T(8,128)(2,1)} %copy-done.6, s16[640,128]{1,0:T(8,128)(2,1)} %copy-done.5, s16[640,128]{1,0:T(8,128)(2,1)} %copy-done.4), custom_call_target="tpu_custom_call" | custom-call | tf_op jit(solution)/shard_map/pallas_call | solution.py:68
  42.5 1.2 %collective-permute-done.9.a3 = s16[8,128,128]{2,1,0:T(8,128)(2,1)S(1)} collective-permute-done((s16[8,128,128]{2,1,0:T(8,128)(2,1)S(1)}, s16[8,128,128]{2,1,0:T(8,128)(2,1)S(1)}, u32[]{:S(2)}, u32[]{:S(2)}) %collective-permute-start.9) | collective-permute-done | bytes 262176 | tf_op jit(solution)/shard_map/ppermute | solution.py:231
  43.7 0.7 copy-done.3
  44.4 11.1 %beams.1 = f32[4,32,4,128]{3,2,1,0:T(4,128)} custom-call(bf16[4,2,1,512,128]{4,3,2,1,0:T(8,128)(2,1)} %shard_map.50.own_steer, bf16[4,2,4,512,128]{4,3,2,1,0:T(8,128)(2,1)} %shard_map.52.col_steer, bf16[4,2,3,512,128]{4,3,2,1,0:T(8,128)(2,1)} %shard_map.51.row_steer, s16[8,128,128]{2,1,0:T(8,128)(2,1)} %copy-done, s16[8,128,128]{2,1,0:T(8,128)(2,1)} %copy-done.1, ...), custom_call_target="tpu_custom_call" | custom-call | tf_op jit(solution)/shard_map/beams/pallas_call | solution.py:132
  55.5 6.6 %all-to-all-start = ((f32[128,4,128]{2,1,0:T(4,128)}), f32[128,4,128]{2,1,0:T(4,128)S(1)}, u32[]{:S(2)}, u32[]{:S(2)}) async-start(f32[128,4,128]{2,1,0:T(4,128)} %bitcast.33), calls=%async_computation | async-start | bytes 524288 | tf_op jit(solution)/shard_map/all_to_all | solution.py:256
  62.8 2.3 %pack.1 = s16[4,3,32,128]{3,2,1,0:T(8,128)(2,1)} custom-call(s32[3]{0:T(128)} %pad_add_fusion.place, s16[8,128,128]{2,1,0:T(8,128)(2,1)} %copy-done, s16[8,128,128]{2,1,0:T(8,128)(2,1)} %copy-done.1, s16[8,128,128]{2,1,0:T(8,128)(2,1)} %copy-done.2, s16[8,128,128]{2,1,0:T(8,128)(2,1)} %copy-done.3), custom_call_target="tpu_custom_call" | custom-call | tf_op jit(solution)/shard_map/pack/pallas_call | solution.py:154
  65.1 2.8 %collective-permute-start.10 = (s16[4,3,32,128]{3,2,1,0:T(8,128)(2,1)}, s16[4,3,32,128]{3,2,1,0:T(8,128)(2,1)S(1)}, u32[]{:S(2)}, u32[]{:S(2)}) collective-permute-start(s16[4,3,32,128]{3,2,1,0:T(8,128)(2,1)} %pack.1), channel_id=1, source_target_pairs={{2,0},{3,1},{4,2},{5,3},{6,4},{7,5},{0,6},{1,7},{10,8},{11,9},{12,... | collective-permute-start | bytes 294920 | tf_op jit(solution)/shard_map/ppermute | solution.py:227
  67.9 3.1 %collective-permute-done.10.rows = s16[4,3,32,128]{3,2,1,0:T(8,128)(2,1)S(1)} collective-permute-done((s16[4,3,32,128]{3,2,1,0:T(8,128)(2,1)}, s16[4,3,32,128]{3,2,1,0:T(8,128)(2,1)S(1)}, u32[]{:S(2)}, u32[]{:S(2)}) %collective-permute-start.10) | collective-permute-done | bytes 98336 | tf_op jit(solution)/shard_map/ppermute | solution.py:227
  71.7 6.3 %tile.1 = bf16[2,4096,128]{2,1,0:T(8,128)(2,1)} custom-call(s32[3]{0:T(128)} %pad_add_fusion.place, s16[4,3,32,128]{3,2,1,0:T(8,128)(2,1)} %copy-done.11, s16[8,128,128]{2,1,0:T(8,128)(2,1)} %copy-done, s16[8,128,128]{2,1,0:T(8,128)(2,1)} %copy-done.1, s16[8,128,128]{2,1,0:T(8,128)(2,1)} %copy-done.2, s16[8,128,128]{2,1,0:T(8,128)(2,1)} %copy-done.3), custom_call_target="tpu_custom_call" | custom-call | tf_op jit(solution)/shard_map/tile/pallas_call | solution.py:208
  (41 shorter events, 3.9 us)
Async XLA Ops:
  2.4 17.5 %collective-permute-start.2 = (s16[640,128]{1,0:T(8,128)(2,1)}, s16[640,128]{1,0:T(8,128)(2,1)S(1)}, u32[]{:S(2)}, u32[]{:S(2)}) collective-permute-start(s16[640,128]{1,0:T(8,128)(2,1)} %prep.1.refs_0_), channel_id=1, source_target_pairs={{24,0},{0,8},{8,16},{16,24},{25,1},{1,9},{9,17},{17,25},{26,2},{2,... | collective-permute-start | bytes 491528 | tf_op jit(solution)/shard_map/ppermute | solution.py:227
  4.0 16.6 %collective-permute-start.1 = (s16[640,128]{1,0:T(8,128)(2,1)}, s16[640,128]{1,0:T(8,128)(2,1)S(1)}, u32[]{:S(2)}, u32[]{:S(2)}) collective-permute-start(s16[640,128]{1,0:T(8,128)(2,1)} %prep.1.refs_0_), channel_id=1, source_target_pairs={{16,0},{24,8},{0,16},{8,24},{17,1},{25,9},{1,17},{9,25},{18,2},{26... | collective-permute-start | bytes 491528 | tf_op jit(solution)/shard_map/ppermute | solution.py:227
  6.8 25.1 %collective-permute-start.6 = (s16[640,128]{1,0:T(8,128)(2,1)}, s16[640,128]{1,0:T(8,128)(2,1)S(1)}, u32[]{:S(2)}, u32[]{:S(2)}) collective-permute-start(s16[640,128]{1,0:T(8,128)(2,1)} %prep.1.refs_0_), channel_id=1, source_target_pairs={{4,0},{5,1},{6,2},{7,3},{0,4},{1,5},{2,6},{3,7},{12,8},{13,9},{14,... | collective-permute-start | bytes 491528 | tf_op jit(solution)/shard_map/ppermute | solution.py:227
  10.6 21.2 %collective-permute-start.5 = (s16[640,128]{1,0:T(8,128)(2,1)}, s16[640,128]{1,0:T(8,128)(2,1)S(1)}, u32[]{:S(2)}, u32[]{:S(2)}) collective-permute-start(s16[640,128]{1,0:T(8,128)(2,1)} %prep.1.refs_0_), channel_id=1, source_target_pairs={{5,0},{6,1},{7,2},{0,3},{1,4},{2,5},{3,6},{4,7},{13,8},{14,9},{15,... | collective-permute-start | bytes 491528 | tf_op jit(solution)/shard_map/ppermute | solution.py:227
  14.3 17.6 %collective-permute-start.4 = (s16[640,128]{1,0:T(8,128)(2,1)}, s16[640,128]{1,0:T(8,128)(2,1)S(1)}, u32[]{:S(2)}, u32[]{:S(2)}) collective-permute-start(s16[640,128]{1,0:T(8,128)(2,1)} %prep.1.refs_0_), channel_id=1, source_target_pairs={{2,0},{3,1},{4,2},{5,3},{6,4},{7,5},{0,6},{1,7},{10,8},{11,9},{12,... | collective-permute-start | bytes 491528 | tf_op jit(solution)/shard_map/ppermute | solution.py:227
  20.0 6.2 %copy-start.8 = (s16[640,128]{1,0:T(8,128)(2,1)}, s16[640,128]{1,0:T(8,128)(2,1)S(1)}, u32[]{:S(2)}) copy-start(s16[640,128]{1,0:T(8,128)(2,1)S(1)} %collective-permute-done.2.refs_2_) | copy-start | bytes 491524
  20.0 11.9 %collective-permute-start.3 = (s16[640,128]{1,0:T(8,128)(2,1)}, s16[640,128]{1,0:T(8,128)(2,1)S(1)}, u32[]{:S(2)}, u32[]{:S(2)}) collective-permute-start(s16[640,128]{1,0:T(8,128)(2,1)} %prep.1.refs_0_), channel_id=1, source_target_pairs={{1,0},{2,1},{3,2},{4,3},{5,4},{6,5},{7,6},{0,7},{9,8},{10,9},{11,1... | collective-permute-start | bytes 491528 | tf_op jit(solution)/shard_map/ppermute | solution.py:227
  20.6 5.5 %copy-start.9 = (s16[640,128]{1,0:T(8,128)(2,1)}, s16[640,128]{1,0:T(8,128)(2,1)S(1)}, u32[]{:S(2)}) copy-start(s16[640,128]{1,0:T(8,128)(2,1)S(1)} %collective-permute-done.1.refs_1_) | copy-start | bytes 491524
  20.6 5.5 %collective-permute-start = (s16[640,128]{1,0:T(8,128)(2,1)}, s16[640,128]{1,0:T(8,128)(2,1)S(1)}, u32[]{:S(2)}, u32[]{:S(2)}) collective-permute-start(s16[640,128]{1,0:T(8,128)(2,1)} %prep.1.refs_0_), channel_id=1, source_target_pairs={{8,0},{16,8},{24,16},{0,24},{9,1},{17,9},{25,17},{1,25},{10,2},{18... | collective-permute-start | bytes 491528 | tf_op jit(solution)/shard_map/ppermute | solution.py:227
  26.1 0.7 copy-start.10
  31.8 4.1 %copy-start.4 = (s16[640,128]{1,0:T(8,128)(2,1)}, s16[640,128]{1,0:T(8,128)(2,1)S(1)}, u32[]{:S(2)}) copy-start(s16[640,128]{1,0:T(8,128)(2,1)S(1)} %collective-permute-done.6.refs_3_) | copy-start | bytes 491524
  31.9 4.1 %copy-start.5 = (s16[640,128]{1,0:T(8,128)(2,1)}, s16[640,128]{1,0:T(8,128)(2,1)S(1)}, u32[]{:S(2)}) copy-start(s16[640,128]{1,0:T(8,128)(2,1)S(1)} %collective-permute-done.5.refs_2_) | copy-start | bytes 491524
  31.9 4.1 %copy-start.6 = (s16[640,128]{1,0:T(8,128)(2,1)}, s16[640,128]{1,0:T(8,128)(2,1)S(1)}, u32[]{:S(2)}) copy-start(s16[640,128]{1,0:T(8,128)(2,1)S(1)} %collective-permute-done.4.refs_1_) | copy-start | bytes 491524
  31.9 4.1 %copy-start.7 = (s16[640,128]{1,0:T(8,128)(2,1)}, s16[640,128]{1,0:T(8,128)(2,1)S(1)}, u32[]{:S(2)}) copy-start(s16[640,128]{1,0:T(8,128)(2,1)S(1)} %collective-permute-done.3.refs_0_) | copy-start | bytes 491524
  34.3 9.4 %copy-start = (s16[8,128,128]{2,1,0:T(8,128)(2,1)}, s16[8,128,128]{2,1,0:T(8,128)(2,1)S(1)}, u32[]{:S(2)}) copy-start(s16[8,128,128]{2,1,0:T(8,128)(2,1)S(1)} %bitcast_dynamic-update-slice_fusion.a0) | copy-start | bytes 786436
  34.3 7.6 %collective-permute-start.7 = (s16[8,128,128]{2,1,0:T(8,128)(2,1)S(1)}, s16[8,128,128]{2,1,0:T(8,128)(2,1)S(1)}, u32[]{:S(2)}, u32[]{:S(2)}) collective-permute-start(s16[8,128,128]{2,1,0:T(8,128)(2,1)S(1)} %bitcast_dynamic-update-slice_fusion.a0), channel_id=1, source_target_pairs={{64,0},{96,32},{0,64},{32,96},{65,1},{97,33},{1,65},{33,97},{66,2}... | collective-permute-start | bytes 786440 | tf_op jit(solution)/shard_map/ppermute | solution.py:231
  36.0 6.6 %collective-permute-start.8 = (s16[8,128,128]{2,1,0:T(8,128)(2,1)S(1)}, s16[8,128,128]{2,1,0:T(8,128)(2,1)S(1)}, u32[]{:S(2)}, u32[]{:S(2)}) collective-permute-start(s16[8,128,128]{2,1,0:T(8,128)(2,1)S(1)} %bitcast_dynamic-update-slice_fusion.a0), channel_id=1, source_target_pairs={{32,0},{0,32},{96,64},{64,96},{33,1},{1,33},{97,65},{65,97},{34,2}... | collective-permute-start | bytes 786440 | tf_op jit(solution)/shard_map/ppermute | solution.py:231
  41.9 1.7 %copy-start.1 = (s16[8,128,128]{2,1,0:T(8,128)(2,1)}, s16[8,128,128]{2,1,0:T(8,128)(2,1)S(1)}, u32[]{:S(2)}) copy-start(s16[8,128,128]{2,1,0:T(8,128)(2,1)S(1)} %collective-permute-done.7.a1) | copy-start | bytes 786436
  42.0 1.7 %collective-permute-start.9 = (s16[8,128,128]{2,1,0:T(8,128)(2,1)S(1)}, s16[8,128,128]{2,1,0:T(8,128)(2,1)S(1)}, u32[]{:S(2)}, u32[]{:S(2)}) collective-permute-start(s16[8,128,128]{2,1,0:T(8,128)(2,1)S(1)} %collective-permute-done.7.a1), channel_id=1, source_target_pairs={{32,0},{0,32},{96,64},{64,96},{33,1},{1,33},{97,65},{65,97},{34,2}... | collective-permute-start | bytes 786440 | tf_op jit(solution)/shard_map/ppermute | solution.py:231
  42.5 1.2 %copy-start.2 = (s16[8,128,128]{2,1,0:T(8,128)(2,1)}, s16[8,128,128]{2,1,0:T(8,128)(2,1)S(1)}, u32[]{:S(2)}) copy-start(s16[8,128,128]{2,1,0:T(8,128)(2,1)S(1)} %collective-permute-done.8.a2) | copy-start | bytes 786436
  43.7 0.7 copy-start.3
  55.5 22.4 %all-to-all-start = ((f32[128,4,128]{2,1,0:T(4,128)}), f32[128,4,128]{2,1,0:T(4,128)S(1)}, u32[]{:S(2)}, u32[]{:S(2)}) async-start(f32[128,4,128]{2,1,0:T(4,128)} %bitcast.33), calls=%async_computation | async-start | bytes 524288 | tf_op jit(solution)/shard_map/all_to_all | solution.py:256
  65.1 5.9 %collective-permute-start.10 = (s16[4,3,32,128]{3,2,1,0:T(8,128)(2,1)}, s16[4,3,32,128]{3,2,1,0:T(8,128)(2,1)S(1)}, u32[]{:S(2)}, u32[]{:S(2)}) collective-permute-start(s16[4,3,32,128]{3,2,1,0:T(8,128)(2,1)} %pack.1), channel_id=1, source_target_pairs={{2,0},{3,1},{4,2},{5,3},{6,4},{7,5},{0,6},{1,7},{10,8},{11,9},{12,... | collective-permute-start | bytes 294920 | tf_op jit(solution)/shard_map/ppermute | solution.py:227
  71.0 0.6 copy-start.11
where the time goes:
time: 80.2 us; the launch traced here: 78.6 us
  Pallas kernels  35.9 us (45%)
  starting transfers between devices  27.8 us (35%)
  waiting for transfers between devices  7.6 us (9%)
  local copies, waits for them, and re-layouts  5.22 us (7%)
  other arithmetic  1.31 us (2%)
    ppermute x8, starting transfers between devices, from_offset(): lax.ppermute(value, axis, [((i + offset) % size, i) for i in range(size)])  19 us
    pallas_call x3, Pallas kernels, steer(): pl.pallas_call(steer_kernel, grid=(NPT // STEP,), out_shape=jax.ShapeDtyp...  14.4 us
    pallas_call x1, Pallas kernels, beams(): pl.pallas_call(beam_kernel, grid=(F,), out_shape=jax.ShapeDtypeStruct((F,...  11.1 us
    all_to_all x1, starting transfers between devices, local(): shares = lax.all_to_all(partial.reshape(128, 4, NST), ALL, 0, 0, tiled=True)  6.62 us
    ppermute x8, waiting for transfers between devices, from_offset(): lax.ppermute(value, axis, [((i + offset) % size, i) for i in range(size)])  6.44 us
    pallas_call x1, Pallas kernels, tile(): pl.pallas_call(tile_kernel, grid_spec=pltpu.PrefetchScalarGridSpec(num_sc...  6.27 us
    unnamed x31, local copies, waits for them, and re-layouts  5.21 us
    pallas_call x1, Pallas kernels, pack(): pl.pallas_call(pack_kernel, grid_spec=pltpu.PrefetchScalarGridSpec(num_sc...  2.25 us
  transfers between devices with their start and end apart: 12, of which 3 were waited for; matrix products, arithmetic and copies ran while one was open for 2% of the time, Pallas kernels for 29%

commit v1 on v0

v1 whole, which is shorter than its diff:
```python
import jax
import jax.numpy as jnp
from jax import lax
from jax.experimental import pallas as pl
from jax.experimental.pallas import tpu as pltpu
from jax.sharding import PartitionSpec as P


S = 4096
NFFT = 4096
F = 4
NST = 128
NPT = 512
ALL = ("win", "srow", "scol")
ROW_OFF = (0, 1, 2, -3, 4)
ROW_WEIGHT = (1.0, 2.0, 2.0, 2.0, 1.0)
RELAY = (4, 6, 7)
ROUND = 12582912.0

ROOT2 = 2.0**0.5
SIN = [ROOT2 * v for v in (3.141592580044453, -5.167706878911761, 2.5500313770692338,
                           -0.5980451729935192, 0.07722012694435497)]
COS = [-ROOT2 * v for v in (0.9999999534664096, -4.93479285864205, 4.058411913501759,
                            -1.331880156986464, 0.2196967900729894)]


def prep_kernel(spectra, travel, payload):
    for f in range(F):
        re = spectra[f, 0]
        im = spectra[f, 1]
        magnitude = jnp.sqrt(re * re + im * im + 0.5)
        for c, part in enumerate((re, im)):
            value = (part / magnitude).astype(jnp.bfloat16).astype(jnp.float32) * 32768.0
            value = jnp.clip((value + ROUND) - ROUND, -32767.0, 32767.0)
            at = NPT + 32 * f + 16 * c
            payload[at:at + 16, :] = value.astype(jnp.int32).astype(jnp.int16)
    payload[0:NPT, :] = travel[...].T.astype(jnp.int16)


def on_chip(*arrays):
    return [pltpu.with_memory_space_constraint(v, pltpu.VMEM) for v in arrays]


def vmem(n):
    return [pl.BlockSpec(memory_space=pltpu.VMEM)] * n


SMEM = pl.BlockSpec(memory_space=pltpu.SMEM)
LIMIT = pltpu.CompilerParams(vmem_limit_bytes=16 * 2**20)


def steer_kernel(bins, *refs):
    payloads, out = refs[:-1], refs[-1]
    rows = 64
    for n, ref in enumerate(payloads):
        def chunk(i, carry, n=n, ref=ref):
            at = pl.ds(pl.multiple_of(i * rows, rows), rows)
            samples = (ref[at, :].astype(jnp.int32) & (NFFT - 1)).astype(jnp.float32)
            for f in range(F):
                scale = bins[f].astype(jnp.float32) * (1.0 / NFFT)
                turns = samples * scale
                r = turns - ((turns + ROUND) - ROUND)
                z = r * r
                s = SIN[4]
                c = COS[4]
                for k in (3, 2, 1, 0):
                    s = s * z + SIN[k]
                    c = c * z + COS[k]
                s = s * r
                out[f, 0, n, at, :] = (1.0 - s * s).astype(jnp.bfloat16)
                out[f, 1, n, at, :] = (s * c).astype(jnp.bfloat16)
            return carry

        lax.fori_loop(0, NPT // rows, chunk, 0)


def steer(bins, payloads):
    n = len(payloads)
    return pl.pallas_call(
        steer_kernel,
        out_shape=pltpu.VMEM((F, 2, n, NPT, NST), jnp.bfloat16),
        in_specs=[SMEM] + vmem(n),
        out_specs=vmem(1)[0],
        compiler_params=LIMIT,
    )(bins, *on_chip(*payloads))


def stack_kernel(*refs):
    for n, ref in enumerate(refs[:-1]):
        refs[-1][n] = ref[NPT:NPT + 32 * F, :]


def stack(payloads):
    return pl.pallas_call(
        stack_kernel,
        out_shape=pltpu.VMEM((len(payloads), 32 * F, NST), jnp.int16),
        in_specs=vmem(len(payloads)),
        out_specs=vmem(1)[0],
        compiler_params=LIMIT,
        name="stack",
    )(*on_chip(*payloads))


def decode(sources, block, f):
    at = pl.ds(pl.multiple_of(32 * f, 32), 32)
    return [
        (a[block, at, :].astype(jnp.int32).astype(jnp.float32) * (1.0 / 32768.0)).astype(jnp.bfloat16)
        for a in sources
    ]


def beam_kernel(own_steer, col_steer, row_steer, a0, a1, a2, a3, beam, cols, weights):
    sources = (a0, a1, a2, a3)

    def one(f, carry):
        for d in range(4):
            cols[d * NST:(d + 1) * NST, :] = jnp.concatenate(decode(sources, d, f), axis=0).T

        def coherent(k):
            parts = decode(sources, 0 if k == 0 else 3 + k, f)
            x = jnp.concatenate(parts, axis=0)
            z = jnp.concatenate([q for v in parts for q in (v[16:32], -v[0:16])], axis=0)
            right = jnp.concatenate([x, z], axis=1)
            for j in range(4):
                at = slice(j * NST, (j + 1) * NST)
                cross = jnp.dot(cols[at, :], right, preferred_element_type=jnp.float32)
                re = cross[:, :NST]
                im = cross[:, NST:]
                inverse = lax.rsqrt(re * re + im * im + 64.0)
                if ROW_WEIGHT[k] != 1.0:
                    inverse = inverse * ROW_WEIGHT[k]
                re = (re * inverse).astype(jnp.bfloat16)
                im = (im * inverse).astype(jnp.bfloat16)
                weights[k, at, :NST] = re
                weights[k, at, NST:] = im
                at = slice((4 + j) * NST, (5 + j) * NST)
                weights[k, at, :NST] = -im
                weights[k, at, NST:] = re

        steer_cols = jnp.concatenate(
            [ref for part in range(2) for ref in (own_steer[f, part, 0], *(row_steer[f, part, n] for n in range(3)))],
            axis=1,
        )
        total = None
        coherent(0)
        for k in range(5):
            if k < 4:
                coherent(k + 1)
            image = jnp.dot(steer_cols, weights[k], preferred_element_type=jnp.float32)
            re, im = (own_steer[f, 0, 0], own_steer[f, 1, 0]) if k == 0 else (col_steer[f, 0, k - 1], col_steer[f, 1, k - 1])
            power = re.astype(jnp.float32) * image[:, :NST] + im.astype(jnp.float32) * image[:, NST:]
            total = power if total is None else total + power
        for j in range(4):
            value = jnp.sum(total[j * NST:(j + 1) * NST, :].T, axis=0, keepdims=True) * (1.0 / S)
            beam[f, :, j, :] = jnp.broadcast_to(value, (32, NST))
        return carry

    lax.fori_loop(0, F, one, 0)


def beams(own_steer, col_steer, row_steer, spectra):
    return pl.pallas_call(
        beam_kernel,
        out_shape=pltpu.VMEM((F, 32, 4, NST), jnp.float32),
        in_specs=vmem(7),
        out_specs=vmem(1)[0],
        scratch_shapes=[
            pltpu.VMEM((4 * NST, NST), jnp.bfloat16),
            pltpu.VMEM((5, 8 * NST, 2 * NST), jnp.bfloat16),
        ],
        compiler_params=LIMIT,
        name="beams",
    )(*on_chip(own_steer, col_steer, row_steer, *spectra))


def pack_kernel(place, a0, a1, a2, a3, rows):
    at = pl.ds(pl.multiple_of(32 * place[0], 32), 32)
    for s, a in enumerate((a0, a1, a2, a3)):
        for n, block in enumerate(RELAY):
            rows[s, n] = a[block, at, :]


def pack(place, spectra):
    return pl.pallas_call(
        pack_kernel,
        out_shape=pltpu.VMEM((4, 3, 32, NST), jnp.int16),
        in_specs=[SMEM] + vmem(4),
        out_specs=vmem(1)[0],
        compiler_params=LIMIT,
        name="pack",
    )(place, *on_chip(*spectra))


def tile_kernel(place, rows, a0, a1, a2, a3, coherence, cols, scratch):
    n = pl.program_id(0)
    sources = (a0, a1, a2, a3)

    @pl.when(n == 0)
    def _():
        for d in range(4):
            parts = decode(sources, d, place[0])
            x = jnp.concatenate(parts, axis=0)
            y = jnp.concatenate([q for v in parts for q in (-v[16:32], v[0:16])], axis=0)
            cols[d] = jnp.concatenate([x, y], axis=1)

    def emit(parts):
        left = jnp.concatenate(parts, axis=0).T
        for d in range(4):
            cross = jnp.dot(left, cols[d], preferred_element_type=jnp.float32)
            re = cross[:, :NST]
            im = cross[:, NST:]
            inverse = lax.rsqrt(re * re + im * im + 64.0)
            at = pl.ds((place[1] + d) & 3, NST, stride=4)
            scratch[0, at, :] = re * inverse
            scratch[1, at, :] = im * inverse
        coherence[0] = scratch[0].astype(jnp.bfloat16)
        coherence[1] = scratch[1].astype(jnp.bfloat16)

    @pl.when(n < 5)
    def _():
        emit(decode(sources, jnp.where(n == 0, 0, n + 3), place[0]))

    @pl.when(n >= 5)
    def _():
        emit(decode([rows.at[k] for k in range(4)], n - 5, 0))


def tile(place, rows, spectra):
    def at(n, place):
        far = jnp.where(n == 3, -3, jnp.where(n < 5, n, jnp.where(n == 5, 3, 5 - n)))
        return (0, (place[2] + far) & 7, 0)

    return pl.pallas_call(
        tile_kernel,
        grid_spec=pltpu.PrefetchScalarGridSpec(
            num_scalar_prefetch=1,
            grid=(8,),
            in_specs=vmem(5),
            out_specs=pl.BlockSpec((2, 4 * NST, NST), at),
            scratch_shapes=[
                pltpu.VMEM((4, NST, 2 * NST), jnp.bfloat16),
                pltpu.VMEM((2, 4 * NST, NST), jnp.float32),
            ],
        ),
        out_shape=jax.ShapeDtypeStruct((2, 4 * 1024, NST), jnp.bfloat16),
        compiler_params=LIMIT,
        name="tile",
    )(place, *on_chip(rows, *spectra))


def from_offset(value, axis, offset):
    size = lax.axis_size(axis)
    return lax.ppermute(value, axis, [((i + offset) % size, i) for i in range(size)])


def from_partner(value, bit):
    return lax.ppermute(value, "win", [(i ^ bit, i) for i in range(4)])


def local(spectra, bins, travel):
    payload = pl.pallas_call(
        prep_kernel,
        out_shape=pltpu.VMEM((NPT + 32 * F, NST), jnp.int16),
        compiler_params=LIMIT,
        name="prep",
    )(spectra, travel)
    place = jnp.stack([lax.axis_index(a) for a in ALL]).astype(jnp.int32)
    by_row = [from_offset(payload, "srow", d) for d in (1, 2, 3)]
    by_col = [from_offset(payload, "scol", d) for d in ROW_OFF[1:]]
    steer0 = steer(bins, [payload])
    steer2 = steer(bins, by_row)
    by_col, steer0, steer2 = lax.optimization_barrier((by_col, steer0, steer2))
    a0 = stack([payload] + by_row + by_col)
    a1 = from_partner(a0, 2)
    a2 = from_partner(a0, 1)
    steer1 = steer(bins, by_col)
    a1, steer1 = lax.optimization_barrier((a1, steer1))
    a3 = from_partner(a1, 1)
    sources = (a0, a1, a2, a3)
    packed = pack(place, sources)
    rows = from_offset(packed, "scol", 2)
    partial = beams(steer0, steer1, steer2, sources)
    shares = lax.all_to_all(partial.reshape(128, 4, NST), ALL, 0, 0, tiled=True)
    coherence = tile(place, rows, sources)
    beam = shares.reshape(4, 32, 4, NST).sum(axis=1).reshape(1, 4 * NPT)
    return coherence.reshape(1, 2, 1024, 4, NST), beam


def solution(mesh):
    placed = (P(None, None, "win", ("srow", "scol")), P(), P(("srow", "scol"), "win"))
    return jax.shard_map(
        local,
        mesh=mesh,
        in_specs=placed,
        out_specs=(P("win", None, "srow", None, "scol"), P("win", None)),
        check_vma=False,
    )
```

time: 80.2 us -> 63.5 us (0.79); the launches traced: 78.6 us -> 62.8 us
  Pallas kernels: 35.9 us -> 24.8 us
  local copies, waits for them, and re-layouts: 5.22 us -> 2.44 us
    pallas_call x6 -> x7, Pallas kernels: 29.6 us -> 19.6 us  [the longest x1 9.51 us: beams(): pl.pallas_call(beam_kernel, out_shape=pltpu.VMEM((F, 32, 4, NST), jnp.flo...]
    unnamed x31 -> x6, local copies, waits for them, and re-layouts: 5.21 us -> 2.44 us
    ppermute x8, waiting for transfers between devices: 6.44 us -> 3.84 us  [from_offset(): lax.ppermute(value, axis, [((i + offset) % size, i) for i in range(size)])]
    ppermute x8, starting transfers between devices: 19 us -> 21.4 us  [from_offset(): lax.ppermute(value, axis, [((i + offset) % size, i) for i in range(size)])]
    ppermute x3, waiting for transfers between devices: 1.16 us -> 3.31 us  [from_partner(): return lax.ppermute(value, 'win', [(i ^ bit, i) for i in range(4)])]
    all_to_all x1, starting transfers between devices: 6.62 us -> 4.88 us  [local(): shares = lax.all_to_all(partial.reshape(128, 4, NST), ALL, 0, 0, tiled=True)]
    ppermute x3, starting transfers between devices: 2.23 us -> 0.76 us  [from_partner(): return lax.ppermute(value, 'win', [(i ^ bit, i) for i in range(4)])]
    pallas_call x1, Pallas kernels: 6.27 us -> 5.12 us  [tile(): pl.pallas_call(tile_kernel, grid_spec=pltpu.PrefetchScalarGridSpec(num_sc...]
  transfers between devices with their start and end apart: 12 -> 12, of which waited for: 3 -> 3; matrix products, arithmetic and copies ran while one was open for 2% -> 0% of each run, Pallas kernels for 29% -> 24%
where the time goes in v1:
time: 63.5 us; the launch traced here: 62.8 us
  starting transfers between devices  27 us (43%)
  Pallas kernels  24.8 us (39%)
  waiting for transfers between devices  7.15 us (11%)
  local copies, waits for them, and re-layouts  2.44 us (4%)
  between operations  0.75 us (1%)
  other arithmetic  0.72 us (1%)
    ppermute x8, starting transfers between devices, from_offset(): lax.ppermute(value, axis, [((i + offset) % size, i) for i in range(size)])  21.4 us
    pallas_call x1, Pallas kernels, beams(): pl.pallas_call(beam_kernel, out_shape=pltpu.VMEM((F, 32, 4, NST), jnp.flo...  9.51 us
    pallas_call x3, Pallas kernels, steer(): pl.pallas_call(steer_kernel, out_shape=pltpu.VMEM((F, 2, n, NPT, NST), jn...  9.43 us
    pallas_call x1, Pallas kernels, tile(): pl.pallas_call(tile_kernel, grid_spec=pltpu.PrefetchScalarGridSpec(num_sc...  5.12 us
    all_to_all x1, starting transfers between devices, local(): shares = lax.all_to_all(partial.reshape(128, 4, NST), ALL, 0, 0, tiled=True)  4.88 us
    ppermute x8, waiting for transfers between devices, from_offset(): lax.ppermute(value, axis, [((i + offset) % size, i) for i in range(size)])  3.84 us
    ppermute x3, waiting for transfers between devices, from_partner(): return lax.ppermute(value, 'win', [(i ^ bit, i) for i in range(4)])  3.31 us
    unnamed x6, local copies, waits for them, and re-layouts  2.44 us
  transfers between devices with their start and end apart: 12, of which 3 were waited for; matrix products, arithmetic and copies ran while one was open for 0% of the time, Pallas kernels for 24%

profile of v1, /device:TPU:0, one launch (start us, length us, event | category | flops | bytes accessed | tf_op | source)
XLA Modules:
  0.0 62.8 jit_solution(9060752056045872694)
XLA Ops:
  0.6 0.9 %copy-done = s32[128,512]{1,0:T(8,128)S(1)} copy-done((s32[128,512]{1,0:T(8,128)S(1)}, s32[128,512]{1,0:T(8,128)}, u32[]{:S(2)}) %copy-start) | copy-done | bytes 262168
  1.6 0.8 %copy-done.1 = f32[4,2,16,128]{3,2,1,0:T(8,128)S(1)} copy-done((f32[4,2,16,128]{3,2,1,0:T(8,128)S(1)}, f32[4,2,16,128]{3,2,1,0:T(8,128)}, u32[]{:S(2)}) %copy-start.1) | copy-done | bytes 65560
  2.4 0.1 prep.1.refs_0_
  2.6 1.7 %collective-permute-start.2 = (s16[640,128]{1,0:T(8,128)(2,1)S(1)}, s16[640,128]{1,0:T(8,128)(2,1)S(1)}, u32[]{:S(2)}, u32[]{:S(2)}) collective-permute-start(s16[640,128]{1,0:T(8,128)(2,1)S(1)} %prep.1.refs_0_), channel_id=1, source_target_pairs={{24,0},{0,8},{8,16},{16,24},{25,1},{1,9},{9,17},{17,25},{26,2},{2,... | collective-permute-start | bytes 491528 | tf_op jit(solution)/shard_map/ppermute | solution.py:253
  4.2 2.7 %collective-permute-start.1 = (s16[640,128]{1,0:T(8,128)(2,1)S(1)}, s16[640,128]{1,0:T(8,128)(2,1)S(1)}, u32[]{:S(2)}, u32[]{:S(2)}) collective-permute-start(s16[640,128]{1,0:T(8,128)(2,1)S(1)} %prep.1.refs_0_), channel_id=1, source_target_pairs={{16,0},{24,8},{0,16},{8,24},{17,1},{25,9},{1,17},{9,25},{18,2},{26... | collective-permute-start | bytes 491528 | tf_op jit(solution)/shard_map/ppermute | solution.py:253
  7.0 3.9 %collective-permute-start.6 = (s16[640,128]{1,0:T(8,128)(2,1)S(1)}, s16[640,128]{1,0:T(8,128)(2,1)S(1)}, u32[]{:S(2)}, u32[]{:S(2)}) collective-permute-start(s16[640,128]{1,0:T(8,128)(2,1)S(1)} %prep.1.refs_0_), channel_id=1, source_target_pairs={{4,0},{5,1},{6,2},{7,3},{0,4},{1,5},{2,6},{3,7},{12,8},{13,9},{14,... | collective-permute-start | bytes 491528 | tf_op jit(solution)/shard_map/ppermute | solution.py:253
  10.8 1.4 %collective-permute-start = (s16[640,128]{1,0:T(8,128)(2,1)S(1)}, s16[640,128]{1,0:T(8,128)(2,1)S(1)}, u32[]{:S(2)}, u32[]{:S(2)}) collective-permute-start(s16[640,128]{1,0:T(8,128)(2,1)S(1)} %prep.1.refs_0_), channel_id=1, source_target_pairs={{8,0},{16,8},{24,16},{0,24},{9,1},{17,9},{25,17},{1,25},{10,2},{18... | collective-permute-start | bytes 491528 | tf_op jit(solution)/shard_map/ppermute | solution.py:253
  12.3 3.6 %collective-permute-start.5 = (s16[640,128]{1,0:T(8,128)(2,1)S(1)}, s16[640,128]{1,0:T(8,128)(2,1)S(1)}, u32[]{:S(2)}, u32[]{:S(2)}) collective-permute-start(s16[640,128]{1,0:T(8,128)(2,1)S(1)} %prep.1.refs_0_), channel_id=1, source_target_pairs={{5,0},{6,1},{7,2},{0,3},{1,4},{2,5},{3,6},{4,7},{13,8},{14,9},{15,... | collective-permute-start | bytes 491528 | tf_op jit(solution)/shard_map/ppermute | solution.py:253
  15.9 2.2 %collective-permute-start.4 = (s16[640,128]{1,0:T(8,128)(2,1)S(1)}, s16[640,128]{1,0:T(8,128)(2,1)S(1)}, u32[]{:S(2)}, u32[]{:S(2)}) collective-permute-start(s16[640,128]{1,0:T(8,128)(2,1)S(1)} %prep.1.refs_0_), channel_id=1, source_target_pairs={{2,0},{3,1},{4,2},{5,3},{6,4},{7,5},{0,6},{1,7},{10,8},{11,9},{12,... | collective-permute-start | bytes 491528 | tf_op jit(solution)/shard_map/ppermute | solution.py:253
  18.1 2.9 %collective-permute-start.3 = (s16[640,128]{1,0:T(8,128)(2,1)S(1)}, s16[640,128]{1,0:T(8,128)(2,1)S(1)}, u32[]{:S(2)}, u32[]{:S(2)}) collective-permute-start(s16[640,128]{1,0:T(8,128)(2,1)S(1)} %prep.1.refs_0_), channel_id=1, source_target_pairs={{1,0},{2,1},{3,2},{4,3},{5,4},{6,5},{7,6},{0,7},{9,8},{10,9},{11,1... | collective-permute-start | bytes 491528 | tf_op jit(solution)/shard_map/ppermute | solution.py:253
  21.1 0.7 %copy-done.2 = s32[4]{0:T(128)S(1)} copy-done((s32[4]{0:T(128)S(1)}, s32[4]{0:T(128)}, u32[]{:S(2)}) %copy-start.2) | copy-done | bytes 40
  21.7 1.5 %shard_map.50.own_steer = bf16[4,2,1,512,128]{4,3,2,1,0:T(8,128)(2,1)S(1)} custom-call(s32[4]{0:T(128)S(1)} %copy-done.2, s16[640,128]{1,0:T(8,128)(2,1)S(1)} %prep.1.refs_0_), custom_call_target="tpu_custom_call" | custom-call | tf_op jit(solution)/shard_map/pallas_call | solution.py:79
  23.2 3.5 %shard_map.51.row_steer = bf16[4,2,3,512,128]{4,3,2,1,0:T(8,128)(2,1)S(1)} custom-call(s32[4]{0:T(128)S(1)} %copy-done.2, s16[640,128]{1,0:T(8,128)(2,1)S(1)} %collective-permute-done.refs_0_.refs_1_, s16[640,128]{1,0:T(8,128)(2,1)S(1)} %collective-permute-done.1.refs_1_.refs_2_, s16[640,128]{1,0:T(8,128)(2,1)S(1)} %collective-permute-done.2.refs_2_.refs_3_), custom_call_target="tpu_custom_call" | custom-call | tf_op jit(solution)/shard_map/pallas_call | solution.py:79
  26.8 0.8 %collective-permute-start.7 = (s16[8,128,128]{2,1,0:T(8,128)(2,1)S(1)}, s16[8,128,128]{2,1,0:T(8,128)(2,1)S(1)}, u32[]{:S(2)}, u32[]{:S(2)}) collective-permute-start(s16[8,128,128]{2,1,0:T(8,128)(2,1)S(1)} %stack.17.a0), channel_id=1, source_target_pairs={{64,0},{96,32},{0,64},{32,96},{65,1},{97,33},{1,65},{33,97},{66,2}... | collective-permute-start | bytes 786440 | tf_op jit(solution)/shard_map/ppermute | solution.py:257
  27.5 4.4 %shard_map.52.col_steer = bf16[4,2,4,512,128]{4,3,2,1,0:T(8,128)(2,1)S(1)} custom-call(s32[4]{0:T(128)S(1)} %copy-done.2, s16[640,128]{1,0:T(8,128)(2,1)S(1)} %collective-permute-done.3.refs_4_.refs_0_, s16[640,128]{1,0:T(8,128)(2,1)S(1)} %collective-permute-done.4.refs_5_.refs_1_, s16[640,128]{1,0:T(8,128)(2,1)S(1)} %collective-permute-done.5.refs_6_.refs_2_, ...), custom_call_target="tpu_custom_call" | custom-call | tf_op jit(solution)/shard_map/pallas_call | solution.py:79
  32.0 1.8 %collective-permute-done.7.a1 = s16[8,128,128]{2,1,0:T(8,128)(2,1)S(1)} collective-permute-done((s16[8,128,128]{2,1,0:T(8,128)(2,1)S(1)}, s16[8,128,128]{2,1,0:T(8,128)(2,1)S(1)}, u32[]{:S(2)}, u32[]{:S(2)}) %collective-permute-start.7) | collective-permute-done | bytes 262176 | tf_op jit(solution)/shard_map/ppermute | solution.py:257
  33.8 1.5 %collective-permute-done.9.a3 = s16[8,128,128]{2,1,0:T(8,128)(2,1)S(1)} collective-permute-done((s16[8,128,128]{2,1,0:T(8,128)(2,1)S(1)}, s16[8,128,128]{2,1,0:T(8,128)(2,1)S(1)}, u32[]{:S(2)}, u32[]{:S(2)}) %collective-permute-start.9) | collective-permute-done | bytes 262176 | tf_op jit(solution)/shard_map/ppermute | solution.py:257
  35.3 9.5 %beams.1 = f32[4,32,4,128]{3,2,1,0:T(4,128)} custom-call(bf16[4,2,1,512,128]{4,3,2,1,0:T(8,128)(2,1)S(1)} %shard_map.50.own_steer, bf16[4,2,4,512,128]{4,3,2,1,0:T(8,128)(2,1)S(1)} %shard_map.52.col_steer, bf16[4,2,3,512,128]{4,3,2,1,0:T(8,128)(2,1)S(1)} %shard_map.51.row_steer, s16[8,128,128]{2,1,0:T(8,128)(2,1)S(1)} %stack.17.a0, ...), custom_call_target="tpu_custom_call" | custom-call | tf_op jit(solution)/shard_map/beams/pallas_call | solution.py:162
  44.8 4.9 %all-to-all-start = ((f32[128,4,128]{2,1,0:T(4,128)}), f32[128,4,128]{2,1,0:T(4,128)S(1)}, u32[]{:S(2)}, u32[]{:S(2)}) async-start(f32[128,4,128]{2,1,0:T(4,128)} %bitcast.4), calls=%async_computation | async-start | bytes 524288 | tf_op jit(solution)/shard_map/all_to_all | solution.py:283
  49.8 0.6 pack.1
  50.4 2.9 %collective-permute-start.10 = (s16[4,3,32,128]{3,2,1,0:T(8,128)(2,1)S(1)}, s16[4,3,32,128]{3,2,1,0:T(8,128)(2,1)S(1)}, u32[]{:S(2)}, u32[]{:S(2)}) collective-permute-start(s16[4,3,32,128]{3,2,1,0:T(8,128)(2,1)S(1)} %pack.1), channel_id=1, source_target_pairs={{2,0},{3,1},{4,2},{5,3},{6,4},{7,5},{0,6},{1,7},{10,8},{11,9},{12,... | collective-permute-start | bytes 294920 | tf_op jit(solution)/shard_map/ppermute | solution.py:253
  53.3 3.8 %collective-permute-done.10.rows = s16[4,3,32,128]{3,2,1,0:T(8,128)(2,1)S(1)} collective-permute-done((s16[4,3,32,128]{3,2,1,0:T(8,128)(2,1)S(1)}, s16[4,3,32,128]{3,2,1,0:T(8,128)(2,1)S(1)}, u32[]{:S(2)}, u32[]{:S(2)}) %collective-permute-start.10) | collective-permute-done | bytes 98336 | tf_op jit(solution)/shard_map/ppermute | solution.py:253
  57.1 5.1 %tile.1 = bf16[2,4096,128]{2,1,0:T(8,128)(2,1)} custom-call(s32[3]{0:T(128)S(1)} %pad_add_fusion.place, s16[4,3,32,128]{3,2,1,0:T(8,128)(2,1)S(1)} %collective-permute-done.10.rows, s16[8,128,128]{2,1,0:T(8,128)(2,1)S(1)} %stack.17.a0, s16[8,128,128]{2,1,0:T(8,128)(2,1)S(1)} %collective-permute-done.7.a1, s16[8,128,128]{2,1,0:T(8,128)(2,1)S(1)} %collective-permute-done.8.a2, ...), custom_call_target="tpu_custom_call" | custom-call | tf_op jit(solution)/shard_map/tile/pallas_call | solution.py:233
  62.2 0.6 %bitcast_reduce_fusion = f32[4,4,128]{2,1,0:T(4,128)} fusion(f32[128,4,128]{2,1,0:T(4,128)S(1)} %all-to-all-done), kind=kLoop, calls=%fused_computation | loop fusion | flops 63488 | bytes 270336 | tf_op jit(solution)/shard_map/reduce_sum | solution.py:285
  (16 shorter events, 0.1 us)
Async XLA Ops:
  0.6 1.0 %copy-start = (s32[128,512]{1,0:T(8,128)S(1)}, s32[128,512]{1,0:T(8,128)}, u32[]{:S(2)}) copy-start(s32[128,512]{1,0:T(8,128)} %travel.1) | copy-start | bytes 786436
  1.6 0.8 %copy-start.1 = (f32[4,2,16,128]{3,2,1,0:T(8,128)S(1)}, f32[4,2,16,128]{3,2,1,0:T(8,128)}, u32[]{:S(2)}) copy-start(f32[4,2,16,128]{3,2,1,0:T(8,128)} %spectra.1) | copy-start | bytes 196612
  2.6 13.4 %collective-permute-start.2 = (s16[640,128]{1,0:T(8,128)(2,1)S(1)}, s16[640,128]{1,0:T(8,128)(2,1)S(1)}, u32[]{:S(2)}, u32[]{:S(2)}) collective-permute-start(s16[640,128]{1,0:T(8,128)(2,1)S(1)} %prep.1.refs_0_), channel_id=1, source_target_pairs={{24,0},{0,8},{8,16},{16,24},{25,1},{1,9},{9,17},{17,25},{26,2},{2,... | collective-permute-start | bytes 491528 | tf_op jit(solution)/shard_map/ppermute | solution.py:253
  4.2 13.9 %collective-permute-start.1 = (s16[640,128]{1,0:T(8,128)(2,1)S(1)}, s16[640,128]{1,0:T(8,128)(2,1)S(1)}, u32[]{:S(2)}, u32[]{:S(2)}) collective-permute-start(s16[640,128]{1,0:T(8,128)(2,1)S(1)} %prep.1.refs_0_), channel_id=1, source_target_pairs={{16,0},{24,8},{0,16},{8,24},{17,1},{25,9},{1,17},{9,25},{18,2},{26... | collective-permute-start | bytes 491528 | tf_op jit(solution)/shard_map/ppermute | solution.py:253
  7.0 19.8 %collective-permute-start.6 = (s16[640,128]{1,0:T(8,128)(2,1)S(1)}, s16[640,128]{1,0:T(8,128)(2,1)S(1)}, u32[]{:S(2)}, u32[]{:S(2)}) collective-permute-start(s16[640,128]{1,0:T(8,128)(2,1)S(1)} %prep.1.refs_0_), channel_id=1, source_target_pairs={{4,0},{5,1},{6,2},{7,3},{0,4},{1,5},{2,6},{3,7},{12,8},{13,9},{14,... | collective-permute-start | bytes 491528 | tf_op jit(solution)/shard_map/ppermute | solution.py:253
  10.8 12.4 %collective-permute-start = (s16[640,128]{1,0:T(8,128)(2,1)S(1)}, s16[640,128]{1,0:T(8,128)(2,1)S(1)}, u32[]{:S(2)}, u32[]{:S(2)}) collective-permute-start(s16[640,128]{1,0:T(8,128)(2,1)S(1)} %prep.1.refs_0_), channel_id=1, source_target_pairs={{8,0},{16,8},{24,16},{0,24},{9,1},{17,9},{25,17},{1,25},{10,2},{18... | collective-permute-start | bytes 491528 | tf_op jit(solution)/shard_map/ppermute | solution.py:253
  12.3 14.5 %collective-permute-start.5 = (s16[640,128]{1,0:T(8,128)(2,1)S(1)}, s16[640,128]{1,0:T(8,128)(2,1)S(1)}, u32[]{:S(2)}, u32[]{:S(2)}) collective-permute-start(s16[640,128]{1,0:T(8,128)(2,1)S(1)} %prep.1.refs_0_), channel_id=1, source_target_pairs={{5,0},{6,1},{7,2},{0,3},{1,4},{2,5},{3,6},{4,7},{13,8},{14,9},{15,... | collective-permute-start | bytes 491528 | tf_op jit(solution)/shard_map/ppermute | solution.py:253
  15.9 10.8 %collective-permute-start.4 = (s16[640,128]{1,0:T(8,128)(2,1)S(1)}, s16[640,128]{1,0:T(8,128)(2,1)S(1)}, u32[]{:S(2)}, u32[]{:S(2)}) collective-permute-start(s16[640,128]{1,0:T(8,128)(2,1)S(1)} %prep.1.refs_0_), channel_id=1, source_target_pairs={{2,0},{3,1},{4,2},{5,3},{6,4},{7,5},{0,6},{1,7},{10,8},{11,9},{12,... | collective-permute-start | bytes 491528 | tf_op jit(solution)/shard_map/ppermute | solution.py:253
  18.1 8.6 %collective-permute-start.3 = (s16[640,128]{1,0:T(8,128)(2,1)S(1)}, s16[640,128]{1,0:T(8,128)(2,1)S(1)}, u32[]{:S(2)}, u32[]{:S(2)}) collective-permute-start(s16[640,128]{1,0:T(8,128)(2,1)S(1)} %prep.1.refs_0_), channel_id=1, source_target_pairs={{1,0},{2,1},{3,2},{4,3},{5,4},{6,5},{7,6},{0,7},{9,8},{10,9},{11,1... | collective-permute-start | bytes 491528 | tf_op jit(solution)/shard_map/ppermute | solution.py:253
  21.1 0.7 %copy-start.2 = (s32[4]{0:T(128)S(1)}, s32[4]{0:T(128)}, u32[]{:S(2)}) copy-start(s32[4]{0:T(128)} %bins.5) | copy-start | bytes 52
  26.8 7.0 %collective-permute-start.7 = (s16[8,128,128]{2,1,0:T(8,128)(2,1)S(1)}, s16[8,128,128]{2,1,0:T(8,128)(2,1)S(1)}, u32[]{:S(2)}, u32[]{:S(2)}) collective-permute-start(s16[8,128,128]{2,1,0:T(8,128)(2,1)S(1)} %stack.17.a0), channel_id=1, source_target_pairs={{64,0},{96,32},{0,64},{32,96},{65,1},{97,33},{1,65},{33,97},{66,2}... | collective-permute-start | bytes 786440 | tf_op jit(solution)/shard_map/ppermute | solution.py:257
  27.5 6.2 %collective-permute-start.8 = (s16[8,128,128]{2,1,0:T(8,128)(2,1)S(1)}, s16[8,128,128]{2,1,0:T(8,128)(2,1)S(1)}, u32[]{:S(2)}, u32[]{:S(2)}) collective-permute-start(s16[8,128,128]{2,1,0:T(8,128)(2,1)S(1)} %stack.17.a0), channel_id=1, source_target_pairs={{32,0},{0,32},{96,64},{64,96},{33,1},{1,33},{97,65},{65,97},{34,2}... | collective-permute-start | bytes 786440 | tf_op jit(solution)/shard_map/ppermute | solution.py:257
  33.8 1.5 %collective-permute-start.9 = (s16[8,128,128]{2,1,0:T(8,128)(2,1)S(1)}, s16[8,128,128]{2,1,0:T(8,128)(2,1)S(1)}, u32[]{:S(2)}, u32[]{:S(2)}) collective-permute-start(s16[8,128,128]{2,1,0:T(8,128)(2,1)S(1)} %collective-permute-done.7.a1), channel_id=1, source_target_pairs={{32,0},{0,32},{96,64},{64,96},{33,1},{1,33},{97,65},{65,97},{34,2}... | collective-permute-start | bytes 786440 | tf_op jit(solution)/shard_map/ppermute | solution.py:257
  44.8 17.4 %all-to-all-start = ((f32[128,4,128]{2,1,0:T(4,128)}), f32[128,4,128]{2,1,0:T(4,128)S(1)}, u32[]{:S(2)}, u32[]{:S(2)}) async-start(f32[128,4,128]{2,1,0:T(4,128)} %bitcast.4), calls=%async_computation | async-start | bytes 524288 | tf_op jit(solution)/shard_map/all_to_all | solution.py:283
  50.4 6.7 %collective-permute-start.10 = (s16[4,3,32,128]{3,2,1,0:T(8,128)(2,1)S(1)}, s16[4,3,32,128]{3,2,1,0:T(8,128)(2,1)S(1)}, u32[]{:S(2)}, u32[]{:S(2)}) collective-permute-start(s16[4,3,32,128]{3,2,1,0:T(8,128)(2,1)S(1)} %pack.1), channel_id=1, source_target_pairs={{2,0},{3,1},{4,2},{5,3},{6,4},{7,5},{0,6},{1,7},{10,8},{11,9},{12,... | collective-permute-start | bytes 294920 | tf_op jit(solution)/shard_map/ppermute | solution.py:253

commit v2 on v1

--- a/solution.py
+++ b/solution.py
@@ -13,7 +13,7 @@
 NPT = 512
 ALL = ("win", "srow", "scol")
 ROW_OFF = (0, 1, 2, -3, 4)
-ROW_WEIGHT = (1.0, 2.0, 2.0, 2.0, 1.0)
+WEIGHT = ((1, 2, 1), (2, 2, 2, 2), (2, 2, 2, 2), (2, 2, 2, 2), (1, 2, 1))
 RELAY = (4, 6, 7)
 ROUND = 12582912.0
 
@@ -82,7 +82,7 @@
         in_specs=[SMEM] + vmem(n),
         out_specs=vmem(1)[0],
         compiler_params=LIMIT,
-    )(bins, *on_chip(*payloads))
+    )(pltpu.with_memory_space_constraint(bins, pltpu.SMEM), *on_chip(*payloads))
 
 
 def stack_kernel(*refs):
@@ -121,24 +121,25 @@
             x = jnp.concatenate(parts, axis=0)
             z = jnp.concatenate([q for v in parts for q in (v[16:32], -v[0:16])], axis=0)
             right = jnp.concatenate([x, z], axis=1)
-            for j in range(4):
+            for j, weight in enumerate(WEIGHT[k]):
                 at = slice(j * NST, (j + 1) * NST)
                 cross = jnp.dot(cols[at, :], right, preferred_element_type=jnp.float32)
                 re = cross[:, :NST]
                 im = cross[:, NST:]
                 inverse = lax.rsqrt(re * re + im * im + 64.0)
-                if ROW_WEIGHT[k] != 1.0:
-                    inverse = inverse * ROW_WEIGHT[k]
+                if weight == 2:
+                    inverse = inverse + inverse
                 re = (re * inverse).astype(jnp.bfloat16)
                 im = (im * inverse).astype(jnp.bfloat16)
+                at = slice(2 * j * NST, (2 * j + 1) * NST)
                 weights[k, at, :NST] = re
                 weights[k, at, NST:] = im
-                at = slice((4 + j) * NST, (5 + j) * NST)
+                at = slice((2 * j + 1) * NST, (2 * j + 2) * NST)
                 weights[k, at, :NST] = -im
                 weights[k, at, NST:] = re
 
         steer_cols = jnp.concatenate(
-            [ref for part in range(2) for ref in (own_steer[f, part, 0], *(row_steer[f, part, n] for n in range(3)))],
+            [own_steer[f, 0, 0], own_steer[f, 1, 0]] + [row_steer[f, part, n] for n in range(3) for part in range(2)],
             axis=1,
         )
         total = None
@@ -146,7 +147,8 @@
         for k in range(5):
             if k < 4:
                 coherent(k + 1)
-            image = jnp.dot(steer_cols, weights[k], preferred_element_type=jnp.float32)
+            depth = 2 * NST * len(WEIGHT[k])
+            image = jnp.dot(steer_cols[:, :depth], weights[k, :depth], preferred_element_type=jnp.float32)
             re, im = (own_steer[f, 0, 0], own_steer[f, 1, 0]) if k == 0 else (col_steer[f, 0, k - 1], col_steer[f, 1, k - 1])
             power = re.astype(jnp.float32) * image[:, :NST] + im.astype(jnp.float32) * image[:, NST:]
             total = power if total is None else total + power
@@ -173,79 +175,75 @@
     )(*on_chip(own_steer, col_steer, row_steer, *spectra))
 
 
-def pack_kernel(place, a0, a1, a2, a3, rows):
-    at = pl.ds(pl.multiple_of(32 * place[0], 32), 32)
+def pack_kernel(a0, a1, a2, a3, rows):
+    at = pl.ds(pl.multiple_of(32 * lax.axis_index("win"), 32), 32)
     for s, a in enumerate((a0, a1, a2, a3)):
         for n, block in enumerate(RELAY):
             rows[s, n] = a[block, at, :]
 
 
-def pack(place, spectra):
+def pack(spectra):
     return pl.pallas_call(
         pack_kernel,
         out_shape=pltpu.VMEM((4, 3, 32, NST), jnp.int16),
-        in_specs=[SMEM] + vmem(4),
+        in_specs=vmem(4),
         out_specs=vmem(1)[0],
         compiler_params=LIMIT,
         name="pack",
-    )(place, *on_chip(*spectra))
-
-
-def tile_kernel(place, rows, a0, a1, a2, a3, coherence, cols, scratch):
-    n = pl.program_id(0)
+    )(*on_chip(*spectra))
+
+
+def tile_kernel(rows, a0, a1, a2, a3, coherence, cols, scratch, ready, sems):
+    w, r, c = (lax.axis_index(a) for a in ALL)
     sources = (a0, a1, a2, a3)
-
-    @pl.when(n == 0)
-    def _():
-        for d in range(4):
-            parts = decode(sources, d, place[0])
-            x = jnp.concatenate(parts, axis=0)
-            y = jnp.concatenate([q for v in parts for q in (-v[16:32], v[0:16])], axis=0)
-            cols[d] = jnp.concatenate([x, y], axis=1)
-
-    def emit(parts):
+    for d in range(4):
+        parts = decode(sources, d, w)
+        x = jnp.concatenate(parts, axis=0)
+        y = jnp.concatenate([q for v in parts for q in (-v[16:32], v[0:16])], axis=0)
+        cols[d] = jnp.concatenate([x, y], axis=1)
+
+    def send(offset, slot):
+        at = pl.ds(pl.multiple_of(((c + offset) & 7) * (4 * NST), 4 * NST), 4 * NST)
+        return pltpu.make_async_copy(ready.at[slot], coherence.at[:, at, :], sems.at[slot])
+
+    def emit(parts, slot):
         left = jnp.concatenate(parts, axis=0).T
         for d in range(4):
             cross = jnp.dot(left, cols[d], preferred_element_type=jnp.float32)
             re = cross[:, :NST]
             im = cross[:, NST:]
             inverse = lax.rsqrt(re * re + im * im + 64.0)
-            at = pl.ds((place[1] + d) & 3, NST, stride=4)
+            at = pl.ds((r + d) & 3, NST, stride=4)
             scratch[0, at, :] = re * inverse
             scratch[1, at, :] = im * inverse
-        coherence[0] = scratch[0].astype(jnp.bfloat16)
-        coherence[1] = scratch[1].astype(jnp.bfloat16)
-
-    @pl.when(n < 5)
-    def _():
-        emit(decode(sources, jnp.where(n == 0, 0, n + 3), place[0]))
-
-    @pl.when(n >= 5)
-    def _():
-        emit(decode([rows.at[k] for k in range(4)], n - 5, 0))
-
-
-def tile(place, rows, spectra):
-    def at(n, place):
-        far = jnp.where(n == 3, -3, jnp.where(n < 5, n, jnp.where(n == 5, 3, 5 - n)))
-        return (0, (place[2] + far) & 7, 0)
-
+        ready[slot, 0] = scratch[0].astype(jnp.bfloat16)
+        ready[slot, 1] = scratch[1].astype(jnp.bfloat16)
+
+    for n, offset in enumerate(ROW_OFF):
+        emit(decode(sources, 0 if n == 0 else 3 + n, w), n)
+        send(offset, n).start()
+    for n, offset in enumerate((3, -1, -2)):
+        emit(decode([rows.at[k] for k in range(4)], n, 0), 5 + n)
+        send(offset, 5 + n).start()
+    for n, offset in enumerate(ROW_OFF + (3, -1, -2)):
+        send(offset, n).wait()
+
+
+def tile(rows, spectra):
     return pl.pallas_call(
         tile_kernel,
-        grid_spec=pltpu.PrefetchScalarGridSpec(
-            num_scalar_prefetch=1,
-            grid=(8,),
-            in_specs=vmem(5),
-            out_specs=pl.BlockSpec((2, 4 * NST, NST), at),
-            scratch_shapes=[
-                pltpu.VMEM((4, NST, 2 * NST), jnp.bfloat16),
-                pltpu.VMEM((2, 4 * NST, NST), jnp.float32),
-            ],
-        ),
+        in_specs=vmem(5),
+        out_specs=pl.BlockSpec(memory_space=pl.ANY),
+        scratch_shapes=[
+            pltpu.VMEM((4, NST, 2 * NST), jnp.bfloat16),
+            pltpu.VMEM((2, 4 * NST, NST), jnp.float32),
+            pltpu.VMEM((8, 2, 4 * NST, NST), jnp.bfloat16),
+            pltpu.SemaphoreType.DMA((8,)),
+        ],
         out_shape=jax.ShapeDtypeStruct((2, 4 * 1024, NST), jnp.bfloat16),
         compiler_params=LIMIT,
         name="tile",
-    )(place, *on_chip(rows, *spectra))
+    )(*on_chip(rows, *spectra))
 
 
 def from_offset(value, axis, offset):
@@ -264,7 +262,6 @@
         compiler_params=LIMIT,
         name="prep",
     )(spectra, travel)
-    place = jnp.stack([lax.axis_index(a) for a in ALL]).astype(jnp.int32)
     by_row = [from_offset(payload, "srow", d) for d in (1, 2, 3)]
     by_col = [from_offset(payload, "scol", d) for d in ROW_OFF[1:]]
     steer0 = steer(bins, [payload])
@@ -277,11 +274,11 @@
     a1, steer1 = lax.optimization_barrier((a1, steer1))
     a3 = from_partner(a1, 1)
     sources = (a0, a1, a2, a3)
-    packed = pack(place, sources)
+    packed = pack(sources)
     rows = from_offset(packed, "scol", 2)
     partial = beams(steer0, steer1, steer2, sources)
     shares = lax.all_to_all(partial.reshape(128, 4, NST), ALL, 0, 0, tiled=True)
-    coherence = tile(place, rows, sources)
+    coherence = tile(rows, sources)
     beam = shares.reshape(4, 32, 4, NST).sum(axis=1).reshape(1, 4 * NPT)
     return coherence.reshape(1, 2, 1024, 4, NST), beam
 

time: 63.5 us -> 60.7 us (0.956)
  Pallas kernels: 24.8 us -> 20.3 us
  waiting for transfers between devices: 7.15 us -> 9.13 us
    pallas_call x1, Pallas kernels: 5.12 us -> 2.1 us  [tile(): pl.pallas_call(tile_kernel, in_specs=vmem(5), out_specs=pl.BlockSpec(memo...]
    all_to_all x1, waiting for transfers between devices: 0.01 us -> 1.66 us  [local(): shares = lax.all_to_all(partial.reshape(128, 4, NST), ALL, 0, 0, tiled=True)]
    pallas_call x1, Pallas kernels: 9.51 us -> 8.62 us  [beams(): pl.pallas_call(beam_kernel, out_shape=pltpu.VMEM((F, 32, 4, NST), jnp.flo...]
  transfers between devices with their start and end apart: 12 -> 12, of which waited for: 3 -> 4; matrix products, arithmetic and copies ran while one was open for 0% -> 0% of each run, Pallas kernels for 24% -> 19%
where the time goes in v2:
time: 60.7 us; the launch traced here: 60.3 us
  starting transfers between devices  27 us (44%)
  Pallas kernels  20.3 us (33%)
  waiting for transfers between devices  9.13 us (15%)
  local copies, waits for them, and re-layouts  2.44 us (4%)
  between operations  0.75 us (1%)
  other arithmetic  0.64 us (1%)
    ppermute x8, starting transfers between devices, from_offset(): lax.ppermute(value, axis, [((i + offset) % size, i) for i in range(size)])  21.4 us
    pallas_call x3, Pallas kernels, steer(): pl.pallas_call(steer_kernel, out_shape=pltpu.VMEM((F, 2, n, NPT, NST), jn...  9.43 us
    pallas_call x1, Pallas kernels, beams(): pl.pallas_call(beam_kernel, out_shape=pltpu.VMEM((F, 32, 4, NST), jnp.flo...  8.62 us
    all_to_all x1, starting transfers between devices, local(): shares = lax.all_to_all(partial.reshape(128, 4, NST), ALL, 0, 0, tiled=True)  4.88 us
    ppermute x8, waiting for transfers between devices, from_offset(): lax.ppermute(value, axis, [((i + offset) % size, i) for i in range(size)])  4.16 us
    ppermute x3, waiting for transfers between devices, from_partner(): return lax.ppermute(value, 'win', [(i ^ bit, i) for i in range(4)])  3.31 us
    unnamed x6, local copies, waits for them, and re-layouts  2.44 us
    pallas_call x1, Pallas kernels, tile(): pl.pallas_call(tile_kernel, in_specs=vmem(5), out_specs=pl.BlockSpec(memo...  2.1 us
  transfers between devices with their start and end apart: 12, of which 4 were waited for; matrix products, arithmetic and copies ran while one was open for 0% of the time, Pallas kernels for 19%

profile of v2, /device:TPU:0, one launch (start us, length us, event | category | flops | bytes accessed | tf_op | source)
XLA Modules:
  0.0 60.3 jit_solution(5733993127904027440)
XLA Ops:
  0.6 0.9 %copy-done = s32[128,512]{1,0:T(8,128)S(1)} copy-done((s32[128,512]{1,0:T(8,128)S(1)}, s32[128,512]{1,0:T(8,128)}, u32[]{:S(2)}) %copy-start) | copy-done | bytes 262168
  1.6 0.8 %copy-done.1 = f32[4,2,16,128]{3,2,1,0:T(8,128)S(1)} copy-done((f32[4,2,16,128]{3,2,1,0:T(8,128)S(1)}, f32[4,2,16,128]{3,2,1,0:T(8,128)}, u32[]{:S(2)}) %copy-start.1) | copy-done | bytes 65560
  2.4 0.1 prep.1.refs_0_
  2.6 1.7 %collective-permute-start.2 = (s16[640,128]{1,0:T(8,128)(2,1)S(1)}, s16[640,128]{1,0:T(8,128)(2,1)S(1)}, u32[]{:S(2)}, u32[]{:S(2)}) collective-permute-start(s16[640,128]{1,0:T(8,128)(2,1)S(1)} %prep.1.refs_0_), channel_id=1, source_target_pairs={{24,0},{0,8},{8,16},{16,24},{25,1},{1,9},{9,17},{17,25},{26,2},{2,... | collective-permute-start | bytes 491528 | tf_op jit(solution)/shard_map/ppermute | solution.py:251
  4.2 2.7 %collective-permute-start.1 = (s16[640,128]{1,0:T(8,128)(2,1)S(1)}, s16[640,128]{1,0:T(8,128)(2,1)S(1)}, u32[]{:S(2)}, u32[]{:S(2)}) collective-permute-start(s16[640,128]{1,0:T(8,128)(2,1)S(1)} %prep.1.refs_0_), channel_id=1, source_target_pairs={{16,0},{24,8},{0,16},{8,24},{17,1},{25,9},{1,17},{9,25},{18,2},{26... | collective-permute-start | bytes 491528 | tf_op jit(solution)/shard_map/ppermute | solution.py:251
  7.0 3.9 %collective-permute-start.6 = (s16[640,128]{1,0:T(8,128)(2,1)S(1)}, s16[640,128]{1,0:T(8,128)(2,1)S(1)}, u32[]{:S(2)}, u32[]{:S(2)}) collective-permute-start(s16[640,128]{1,0:T(8,128)(2,1)S(1)} %prep.1.refs_0_), channel_id=1, source_target_pairs={{4,0},{5,1},{6,2},{7,3},{0,4},{1,5},{2,6},{3,7},{12,8},{13,9},{14,... | collective-permute-start | bytes 491528 | tf_op jit(solution)/shard_map/ppermute | solution.py:251
  10.8 1.4 %collective-permute-start = (s16[640,128]{1,0:T(8,128)(2,1)S(1)}, s16[640,128]{1,0:T(8,128)(2,1)S(1)}, u32[]{:S(2)}, u32[]{:S(2)}) collective-permute-start(s16[640,128]{1,0:T(8,128)(2,1)S(1)} %prep.1.refs_0_), channel_id=1, source_target_pairs={{8,0},{16,8},{24,16},{0,24},{9,1},{17,9},{25,17},{1,25},{10,2},{18... | collective-permute-start | bytes 491528 | tf_op jit(solution)/shard_map/ppermute | solution.py:251
  12.3 3.6 %collective-permute-start.5 = (s16[640,128]{1,0:T(8,128)(2,1)S(1)}, s16[640,128]{1,0:T(8,128)(2,1)S(1)}, u32[]{:S(2)}, u32[]{:S(2)}) collective-permute-start(s16[640,128]{1,0:T(8,128)(2,1)S(1)} %prep.1.refs_0_), channel_id=1, source_target_pairs={{5,0},{6,1},{7,2},{0,3},{1,4},{2,5},{3,6},{4,7},{13,8},{14,9},{15,... | collective-permute-start | bytes 491528 | tf_op jit(solution)/shard_map/ppermute | solution.py:251
  15.9 2.2 %collective-permute-start.4 = (s16[640,128]{1,0:T(8,128)(2,1)S(1)}, s16[640,128]{1,0:T(8,128)(2,1)S(1)}, u32[]{:S(2)}, u32[]{:S(2)}) collective-permute-start(s16[640,128]{1,0:T(8,128)(2,1)S(1)} %prep.1.refs_0_), channel_id=1, source_target_pairs={{2,0},{3,1},{4,2},{5,3},{6,4},{7,5},{0,6},{1,7},{10,8},{11,9},{12,... | collective-permute-start | bytes 491528 | tf_op jit(solution)/shard_map/ppermute | solution.py:251
  18.1 2.9 %collective-permute-start.3 = (s16[640,128]{1,0:T(8,128)(2,1)S(1)}, s16[640,128]{1,0:T(8,128)(2,1)S(1)}, u32[]{:S(2)}, u32[]{:S(2)}) collective-permute-start(s16[640,128]{1,0:T(8,128)(2,1)S(1)} %prep.1.refs_0_), channel_id=1, source_target_pairs={{1,0},{2,1},{3,2},{4,3},{5,4},{6,5},{7,6},{0,7},{9,8},{10,9},{11,1... | collective-permute-start | bytes 491528 | tf_op jit(solution)/shard_map/ppermute | solution.py:251
  21.1 0.7 %copy-done.2 = s32[4]{0:T(128)S(1)} copy-done((s32[4]{0:T(128)S(1)}, s32[4]{0:T(128)}, u32[]{:S(2)}) %copy-start.2) | copy-done | bytes 40
  21.7 1.5 %shard_map.50.own_steer = bf16[4,2,1,512,128]{4,3,2,1,0:T(8,128)(2,1)S(1)} custom-call(s32[4]{0:T(128)S(1)} %copy-done.2, s16[640,128]{1,0:T(8,128)(2,1)S(1)} %prep.1.refs_0_), custom_call_target="tpu_custom_call" | custom-call | tf_op jit(solution)/shard_map/pallas_call | solution.py:79
  23.2 3.5 %shard_map.51.row_steer = bf16[4,2,3,512,128]{4,3,2,1,0:T(8,128)(2,1)S(1)} custom-call(s32[4]{0:T(128)S(1)} %copy-done.2, s16[640,128]{1,0:T(8,128)(2,1)S(1)} %collective-permute-done.refs_0_.refs_1_, s16[640,128]{1,0:T(8,128)(2,1)S(1)} %collective-permute-done.1.refs_1_.refs_2_, s16[640,128]{1,0:T(8,128)(2,1)S(1)} %collective-permute-done.2.refs_2_.refs_3_), custom_call_target="tpu_custom_call" | custom-call | tf_op jit(solution)/shard_map/pallas_call | solution.py:79
  26.8 0.8 %collective-permute-start.7 = (s16[8,128,128]{2,1,0:T(8,128)(2,1)S(1)}, s16[8,128,128]{2,1,0:T(8,128)(2,1)S(1)}, u32[]{:S(2)}, u32[]{:S(2)}) collective-permute-start(s16[8,128,128]{2,1,0:T(8,128)(2,1)S(1)} %stack.1.a0), channel_id=1, source_target_pairs={{64,0},{96,32},{0,64},{32,96},{65,1},{97,33},{1,65},{33,97},{66,2}... | collective-permute-start | bytes 786440 | tf_op jit(solution)/shard_map/ppermute | solution.py:255
  27.5 4.4 %shard_map.52.col_steer = bf16[4,2,4,512,128]{4,3,2,1,0:T(8,128)(2,1)S(1)} custom-call(s32[4]{0:T(128)S(1)} %copy-done.2, s16[640,128]{1,0:T(8,128)(2,1)S(1)} %collective-permute-done.3.refs_4_.refs_0_, s16[640,128]{1,0:T(8,128)(2,1)S(1)} %collective-permute-done.4.refs_5_.refs_1_, s16[640,128]{1,0:T(8,128)(2,1)S(1)} %collective-permute-done.5.refs_6_.refs_2_, ...), custom_call_target="tpu_custom_call" | custom-call | tf_op jit(solution)/shard_map/pallas_call | solution.py:79
  32.0 1.8 %collective-permute-done.7.a1 = s16[8,128,128]{2,1,0:T(8,128)(2,1)S(1)} collective-permute-done((s16[8,128,128]{2,1,0:T(8,128)(2,1)S(1)}, s16[8,128,128]{2,1,0:T(8,128)(2,1)S(1)}, u32[]{:S(2)}, u32[]{:S(2)}) %collective-permute-start.7) | collective-permute-done | bytes 262176 | tf_op jit(solution)/shard_map/ppermute | solution.py:255
  33.8 1.5 %collective-permute-done.9.a3 = s16[8,128,128]{2,1,0:T(8,128)(2,1)S(1)} collective-permute-done((s16[8,128,128]{2,1,0:T(8,128)(2,1)S(1)}, s16[8,128,128]{2,1,0:T(8,128)(2,1)S(1)}, u32[]{:S(2)}, u32[]{:S(2)}) %collective-permute-start.9) | collective-permute-done | bytes 262176 | tf_op jit(solution)/shard_map/ppermute | solution.py:255
  35.3 8.6 %beams.1 = f32[4,32,4,128]{3,2,1,0:T(4,128)} custom-call(bf16[4,2,1,512,128]{4,3,2,1,0:T(8,128)(2,1)S(1)} %shard_map.50.own_steer, bf16[4,2,4,512,128]{4,3,2,1,0:T(8,128)(2,1)S(1)} %shard_map.52.col_steer, bf16[4,2,3,512,128]{4,3,2,1,0:T(8,128)(2,1)S(1)} %shard_map.51.row_steer, s16[8,128,128]{2,1,0:T(8,128)(2,1)S(1)} %stack.1.a0, ...), custom_call_target="tpu_custom_call" | custom-call | tf_op jit(solution)/shard_map/beams/pallas_call | solution.py:164
  43.9 4.9 %all-to-all-start = ((f32[128,4,128]{2,1,0:T(4,128)}), f32[128,4,128]{2,1,0:T(4,128)S(1)}, u32[]{:S(2)}, u32[]{:S(2)}) async-start(f32[128,4,128]{2,1,0:T(4,128)} %bitcast.1), calls=%async_computation | async-start | bytes 524288 | tf_op jit(solution)/shard_map/all_to_all | solution.py:280
  48.8 2.9 %collective-permute-start.10 = (s16[4,3,32,128]{3,2,1,0:T(8,128)(2,1)S(1)}, s16[4,3,32,128]{3,2,1,0:T(8,128)(2,1)S(1)}, u32[]{:S(2)}, u32[]{:S(2)}) collective-permute-start(s16[4,3,32,128]{3,2,1,0:T(8,128)(2,1)S(1)} %pack.1), channel_id=1, source_target_pairs={{2,0},{3,1},{4,2},{5,3},{6,4},{7,5},{0,6},{1,7},{10,8},{11,9},{12,... | collective-permute-start | bytes 294920 | tf_op jit(solution)/shard_map/ppermute | solution.py:251
  51.7 4.1 %collective-permute-done.10.rows = s16[4,3,32,128]{3,2,1,0:T(8,128)(2,1)S(1)} collective-permute-done((s16[4,3,32,128]{3,2,1,0:T(8,128)(2,1)S(1)}, s16[4,3,32,128]{3,2,1,0:T(8,128)(2,1)S(1)}, u32[]{:S(2)}, u32[]{:S(2)}) %collective-permute-start.10) | collective-permute-done | bytes 98336 | tf_op jit(solution)/shard_map/ppermute | solution.py:251
  55.9 2.1 %tile.1 = bf16[2,4096,128]{2,1,0:T(8,128)(2,1)} custom-call(s16[4,3,32,128]{3,2,1,0:T(8,128)(2,1)S(1)} %collective-permute-done.10.rows, s16[8,128,128]{2,1,0:T(8,128)(2,1)S(1)} %stack.1.a0, s16[8,128,128]{2,1,0:T(8,128)(2,1)S(1)} %collective-permute-done.7.a1, s16[8,128,128]{2,1,0:T(8,128)(2,1)S(1)} %collective-permute-done.8.a2, ...), custom_call_target="tpu_custom_call" | custom-call | tf_op jit(solution)/shard_map/tile/pallas_call | solution.py:233
  58.0 1.7 %all-to-all-done = f32[128,4,128]{2,1,0:T(4,128)S(1)} async-done(((f32[128,4,128]{2,1,0:T(4,128)}), f32[128,4,128]{2,1,0:T(4,128)S(1)}, u32[]{:S(2)}, u32[]{:S(2)}) %all-to-all-start) | async-done | bytes 262176 | tf_op jit(solution)/shard_map/all_to_all | solution.py:280
  59.7 0.6 %bitcast_reduce_fusion = f32[4,4,128]{2,1,0:T(4,128)} fusion(f32[128,4,128]{2,1,0:T(4,128)S(1)} %all-to-all-done), kind=kLoop, calls=%fused_computation | loop fusion | flops 63488 | bytes 270336 | tf_op jit(solution)/shard_map/reduce_sum | solution.py:282
  (15 shorter events, 0.1 us)
Async XLA Ops:
  0.6 1.0 %copy-start = (s32[128,512]{1,0:T(8,128)S(1)}, s32[128,512]{1,0:T(8,128)}, u32[]{:S(2)}) copy-start(s32[128,512]{1,0:T(8,128)} %travel.1) | copy-start | bytes 786436
  1.6 0.8 %copy-start.1 = (f32[4,2,16,128]{3,2,1,0:T(8,128)S(1)}, f32[4,2,16,128]{3,2,1,0:T(8,128)}, u32[]{:S(2)}) copy-start(f32[4,2,16,128]{3,2,1,0:T(8,128)} %spectra.1) | copy-start | bytes 196612
  2.6 13.4 %collective-permute-start.2 = (s16[640,128]{1,0:T(8,128)(2,1)S(1)}, s16[640,128]{1,0:T(8,128)(2,1)S(1)}, u32[]{:S(2)}, u32[]{:S(2)}) collective-permute-start(s16[640,128]{1,0:T(8,128)(2,1)S(1)} %prep.1.refs_0_), channel_id=1, source_target_pairs={{24,0},{0,8},{8,16},{16,24},{25,1},{1,9},{9,17},{17,25},{26,2},{2,... | collective-permute-start | bytes 491528 | tf_op jit(solution)/shard_map/ppermute | solution.py:251
  4.2 13.9 %collective-permute-start.1 = (s16[640,128]{1,0:T(8,128)(2,1)S(1)}, s16[640,128]{1,0:T(8,128)(2,1)S(1)}, u32[]{:S(2)}, u32[]{:S(2)}) collective-permute-start(s16[640,128]{1,0:T(8,128)(2,1)S(1)} %prep.1.refs_0_), channel_id=1, source_target_pairs={{16,0},{24,8},{0,16},{8,24},{17,1},{25,9},{1,17},{9,25},{18,2},{26... | collective-permute-start | bytes 491528 | tf_op jit(solution)/shard_map/ppermute | solution.py:251
  7.0 19.8 %collective-permute-start.6 = (s16[640,128]{1,0:T(8,128)(2,1)S(1)}, s16[640,128]{1,0:T(8,128)(2,1)S(1)}, u32[]{:S(2)}, u32[]{:S(2)}) collective-permute-start(s16[640,128]{1,0:T(8,128)(2,1)S(1)} %prep.1.refs_0_), channel_id=1, source_target_pairs={{4,0},{5,1},{6,2},{7,3},{0,4},{1,5},{2,6},{3,7},{12,8},{13,9},{14,... | collective-permute-start | bytes 491528 | tf_op jit(solution)/shard_map/ppermute | solution.py:251
  10.8 12.4 %collective-permute-start = (s16[640,128]{1,0:T(8,128)(2,1)S(1)}, s16[640,128]{1,0:T(8,128)(2,1)S(1)}, u32[]{:S(2)}, u32[]{:S(2)}) collective-permute-start(s16[640,128]{1,0:T(8,128)(2,1)S(1)} %prep.1.refs_0_), channel_id=1, source_target_pairs={{8,0},{16,8},{24,16},{0,24},{9,1},{17,9},{25,17},{1,25},{10,2},{18... | collective-permute-start | bytes 491528 | tf_op jit(solution)/shard_map/ppermute | solution.py:251
  12.3 14.5 %collective-permute-start.5 = (s16[640,128]{1,0:T(8,128)(2,1)S(1)}, s16[640,128]{1,0:T(8,128)(2,1)S(1)}, u32[]{:S(2)}, u32[]{:S(2)}) collective-permute-start(s16[640,128]{1,0:T(8,128)(2,1)S(1)} %prep.1.refs_0_), channel_id=1, source_target_pairs={{5,0},{6,1},{7,2},{0,3},{1,4},{2,5},{3,6},{4,7},{13,8},{14,9},{15,... | collective-permute-start | bytes 491528 | tf_op jit(solution)/shard_map/ppermute | solution.py:251
  15.9 10.8 %collective-permute-start.4 = (s16[640,128]{1,0:T(8,128)(2,1)S(1)}, s16[640,128]{1,0:T(8,128)(2,1)S(1)}, u32[]{:S(2)}, u32[]{:S(2)}) collective-permute-start(s16[640,128]{1,0:T(8,128)(2,1)S(1)} %prep.1.refs_0_), channel_id=1, source_target_pairs={{2,0},{3,1},{4,2},{5,3},{6,4},{7,5},{0,6},{1,7},{10,8},{11,9},{12,... | collective-permute-start | bytes 491528 | tf_op jit(solution)/shard_map/ppermute | solution.py:251
  18.1 8.6 %collective-permute-start.3 = (s16[640,128]{1,0:T(8,128)(2,1)S(1)}, s16[640,128]{1,0:T(8,128)(2,1)S(1)}, u32[]{:S(2)}, u32[]{:S(2)}) collective-permute-start(s16[640,128]{1,0:T(8,128)(2,1)S(1)} %prep.1.refs_0_), channel_id=1, source_target_pairs={{1,0},{2,1},{3,2},{4,3},{5,4},{6,5},{7,6},{0,7},{9,8},{10,9},{11,1... | collective-permute-start | bytes 491528 | tf_op jit(solution)/shard_map/ppermute | solution.py:251
  21.1 0.7 %copy-start.2 = (s32[4]{0:T(128)S(1)}, s32[4]{0:T(128)}, u32[]{:S(2)}) copy-start(s32[4]{0:T(128)} %bins.5) | copy-start | bytes 52
  26.8 7.0 %collective-permute-start.7 = (s16[8,128,128]{2,1,0:T(8,128)(2,1)S(1)}, s16[8,128,128]{2,1,0:T(8,128)(2,1)S(1)}, u32[]{:S(2)}, u32[]{:S(2)}) collective-permute-start(s16[8,128,128]{2,1,0:T(8,128)(2,1)S(1)} %stack.1.a0), channel_id=1, source_target_pairs={{64,0},{96,32},{0,64},{32,96},{65,1},{97,33},{1,65},{33,97},{66,2}... | collective-permute-start | bytes 786440 | tf_op jit(solution)/shard_map/ppermute | solution.py:255
  27.5 6.2 %collective-permute-start.8 = (s16[8,128,128]{2,1,0:T(8,128)(2,1)S(1)}, s16[8,128,128]{2,1,0:T(8,128)(2,1)S(1)}, u32[]{:S(2)}, u32[]{:S(2)}) collective-permute-start(s16[8,128,128]{2,1,0:T(8,128)(2,1)S(1)} %stack.1.a0), channel_id=1, source_target_pairs={{32,0},{0,32},{96,64},{64,96},{33,1},{1,33},{97,65},{65,97},{34,2}... | collective-permute-start | bytes 786440 | tf_op jit(solution)/shard_map/ppermute | solution.py:255
  33.8 1.5 %collective-permute-start.9 = (s16[8,128,128]{2,1,0:T(8,128)(2,1)S(1)}, s16[8,128,128]{2,1,0:T(8,128)(2,1)S(1)}, u32[]{:S(2)}, u32[]{:S(2)}) collective-permute-start(s16[8,128,128]{2,1,0:T(8,128)(2,1)S(1)} %collective-permute-done.7.a1), channel_id=1, source_target_pairs={{32,0},{0,32},{96,64},{64,96},{33,1},{1,33},{97,65},{65,97},{34,2}... | collective-permute-start | bytes 786440 | tf_op jit(solution)/shard_map/ppermute | solution.py:255
  43.9 15.7 %all-to-all-start = ((f32[128,4,128]{2,1,0:T(4,128)}), f32[128,4,128]{2,1,0:T(4,128)S(1)}, u32[]{:S(2)}, u32[]{:S(2)}) async-start(f32[128,4,128]{2,1,0:T(4,128)} %bitcast.1), calls=%async_computation | async-start | bytes 524288 | tf_op jit(solution)/shard_map/all_to_all | solution.py:280
  48.8 7.0 %collective-permute-start.10 = (s16[4,3,32,128]{3,2,1,0:T(8,128)(2,1)S(1)}, s16[4,3,32,128]{3,2,1,0:T(8,128)(2,1)S(1)}, u32[]{:S(2)}, u32[]{:S(2)}) collective-permute-start(s16[4,3,32,128]{3,2,1,0:T(8,128)(2,1)S(1)} %pack.1), channel_id=1, source_target_pairs={{2,0},{3,1},{4,2},{5,3},{6,4},{7,5},{0,6},{1,7},{10,8},{11,9},{12,... | collective-permute-start | bytes 294920 | tf_op jit(solution)/shard_map/ppermute | solution.py:251

commit v3 on v2

--- a/solution.py
+++ b/solution.py
@@ -4,7 +4,6 @@
 from jax.experimental import pallas as pl
 from jax.experimental.pallas import tpu as pltpu
 from jax.sharding import PartitionSpec as P
-
 
 S = 4096
 NFFT = 4096
@@ -24,7 +23,14 @@
                             -1.331880156986464, 0.2196967900729894)]
 
 
-def prep_kernel(spectra, travel, payload):
+def prep_kernel(spectra_hbm, travel_hbm, payload, spectra, travel, sems):
+    moves = [
+        pltpu.make_async_copy(spectra_hbm, spectra, sems.at[0]),
+        pltpu.make_async_copy(travel_hbm, travel, sems.at[1]),
+    ]
+    for move in moves:
+        move.start()
+    moves[0].wait()
     for f in range(F):
         re = spectra[f, 0]
         im = spectra[f, 1]
@@ -34,6 +40,7 @@
             value = jnp.clip((value + ROUND) - ROUND, -32767.0, 32767.0)
             at = NPT + 32 * f + 16 * c
             payload[at:at + 16, :] = value.astype(jnp.int32).astype(jnp.int16)
+    moves[1].wait()
     payload[0:NPT, :] = travel[...].T.astype(jnp.int16)
 
 
@@ -193,57 +200,91 @@
     )(*on_chip(*spectra))
 
 
-def tile_kernel(rows, a0, a1, a2, a3, coherence, cols, scratch, ready, sems):
-    w, r, c = (lax.axis_index(a) for a in ALL)
-    sources = (a0, a1, a2, a3)
+def fill_columns(sources, f, cols):
     for d in range(4):
-        parts = decode(sources, d, w)
+        parts = decode(sources, d, f)
         x = jnp.concatenate(parts, axis=0)
         y = jnp.concatenate([q for v in parts for q in (-v[16:32], v[0:16])], axis=0)
         cols[d] = jnp.concatenate([x, y], axis=1)
 
-    def send(offset, slot):
-        at = pl.ds(pl.multiple_of(((c + offset) & 7) * (4 * NST), 4 * NST), 4 * NST)
-        return pltpu.make_async_copy(ready.at[slot], coherence.at[:, at, :], sems.at[slot])
-
-    def emit(parts, slot):
-        left = jnp.concatenate(parts, axis=0).T
-        for d in range(4):
-            cross = jnp.dot(left, cols[d], preferred_element_type=jnp.float32)
-            re = cross[:, :NST]
-            im = cross[:, NST:]
-            inverse = lax.rsqrt(re * re + im * im + 64.0)
-            at = pl.ds((r + d) & 3, NST, stride=4)
-            scratch[0, at, :] = re * inverse
-            scratch[1, at, :] = im * inverse
-        ready[slot, 0] = scratch[0].astype(jnp.bfloat16)
-        ready[slot, 1] = scratch[1].astype(jnp.bfloat16)
-
+
+def emit(parts, cols, r, scratch, ready):
+    left = jnp.concatenate(parts, axis=0).T
+    for d in range(4):
+        cross = jnp.dot(left, cols[d], preferred_element_type=jnp.float32)
+        re = cross[:, :NST]
+        im = cross[:, NST:]
+        inverse = lax.rsqrt(re * re + im * im + 64.0)
+        at = pl.ds((r + d) & 3, NST, stride=4)
+        scratch[0, at, :] = re * inverse
+        scratch[1, at, :] = im * inverse
+    ready[0] = scratch[0].astype(jnp.bfloat16)
+    ready[1] = scratch[1].astype(jnp.bfloat16)
+
+
+def block_copy(ready, coherence, offset, sem):
+    row = (lax.axis_index("scol") + offset) & 7
+    at = pl.ds(pl.multiple_of(row * (4 * NST), 4 * NST), 4 * NST)
+    return pltpu.make_async_copy(ready, coherence.at[:, at, :], sem)
+
+
+def near_kernel(a0, a1, a2, a3, coherence, cols, scratch, ready, sems):
+    w, r = lax.axis_index("win"), lax.axis_index("srow")
+    sources = (a0, a1, a2, a3)
+    fill_columns(sources, w, cols)
     for n, offset in enumerate(ROW_OFF):
-        emit(decode(sources, 0 if n == 0 else 3 + n, w), n)
-        send(offset, n).start()
+        emit(decode(sources, 0 if n == 0 else 3 + n, w), cols, r, scratch, ready.at[n])
+        block_copy(ready.at[n], coherence, offset, sems.at[n]).start()
+    for n, offset in enumerate(ROW_OFF):
+        block_copy(ready.at[n], coherence, offset, sems.at[n]).wait()
+
+
+def far_kernel(rows, a0, a1, a2, a3, old, coherence, cols, scratch, ready, sems):
+    w, r = lax.axis_index("win"), lax.axis_index("srow")
+    fill_columns((a0, a1, a2, a3), w, cols)
     for n, offset in enumerate((3, -1, -2)):
-        emit(decode([rows.at[k] for k in range(4)], n, 0), 5 + n)
-        send(offset, 5 + n).start()
-    for n, offset in enumerate(ROW_OFF + (3, -1, -2)):
-        send(offset, n).wait()
-
-
-def tile(rows, spectra):
-    return pl.pallas_call(
-        tile_kernel,
-        in_specs=vmem(5),
-        out_specs=pl.BlockSpec(memory_space=pl.ANY),
-        scratch_shapes=[
-            pltpu.VMEM((4, NST, 2 * NST), jnp.bfloat16),
-            pltpu.VMEM((2, 4 * NST, NST), jnp.float32),
-            pltpu.VMEM((8, 2, 4 * NST, NST), jnp.bfloat16),
-            pltpu.SemaphoreType.DMA((8,)),
-        ],
-        out_shape=jax.ShapeDtypeStruct((2, 4 * 1024, NST), jnp.bfloat16),
-        compiler_params=LIMIT,
-        name="tile",
-    )(*on_chip(rows, *spectra))
+        emit(decode([rows.at[k] for k in range(4)], n, 0), cols, r, scratch, ready.at[n])
+        block_copy(ready.at[n], coherence, offset, sems.at[n]).start()
+    for n, offset in enumerate((3, -1, -2)):
+        block_copy(ready.at[n], coherence, offset, sems.at[n]).wait()
+
+
+def tile_scratch(n):
+    return [
+        pltpu.VMEM((4, NST, 2 * NST), jnp.bfloat16),
+        pltpu.VMEM((2, 4 * NST, NST), jnp.float32),
+        pltpu.VMEM((n, 2, 4 * NST, NST), jnp.bfloat16),
+        pltpu.SemaphoreType.DMA((n,)),
+    ]
+
+
+TILE = jax.ShapeDtypeStruct((2, 4 * 1024, NST), jnp.bfloat16)
+ANY = pl.BlockSpec(memory_space=pl.ANY)
+
+
+def near_tile(spectra):
+    return pl.pallas_call(
+        near_kernel,
+        in_specs=vmem(4),
+        out_specs=ANY,
+        scratch_shapes=tile_scratch(5),
+        out_shape=TILE,
+        compiler_params=LIMIT,
+        name="near",
+    )(*on_chip(*spectra))
+
+
+def far_tile(rows, spectra, coherence):
+    return pl.pallas_call(
+        far_kernel,
+        in_specs=vmem(5) + [ANY],
+        out_specs=ANY,
+        scratch_shapes=tile_scratch(3),
+        out_shape=TILE,
+        input_output_aliases={5: 0},
+        compiler_params=LIMIT,
+        name="far",
+    )(*on_chip(rows, *spectra), coherence)
 
 
 def from_offset(value, axis, offset):
@@ -259,9 +300,16 @@
     payload = pl.pallas_call(
         prep_kernel,
         out_shape=pltpu.VMEM((NPT + 32 * F, NST), jnp.int16),
+        in_specs=[pl.BlockSpec(memory_space=pl.ANY)] * 2,
+        out_specs=vmem(1)[0],
+        scratch_shapes=[
+            pltpu.VMEM(spectra.shape, jnp.float32),
+            pltpu.VMEM(travel.shape, jnp.int32),
+            pltpu.SemaphoreType.DMA((2,)),
+        ],
         compiler_params=LIMIT,
         name="prep",
-    )(spectra, travel)
+    )(*(pltpu.with_memory_space_constraint(v, pltpu.HBM) for v in (spectra, travel)))
     by_row = [from_offset(payload, "srow", d) for d in (1, 2, 3)]
     by_col = [from_offset(payload, "scol", d) for d in ROW_OFF[1:]]
     steer0 = steer(bins, [payload])
@@ -278,7 +326,7 @@
     rows = from_offset(packed, "scol", 2)
     partial = beams(steer0, steer1, steer2, sources)
     shares = lax.all_to_all(partial.reshape(128, 4, NST), ALL, 0, 0, tiled=True)
-    coherence = tile(rows, sources)
+    coherence = far_tile(rows, sources, near_tile(sources))
     beam = shares.reshape(4, 32, 4, NST).sum(axis=1).reshape(1, 4 * NPT)
     return coherence.reshape(1, 2, 1024, 4, NST), beam
 

time: 60.7 us -> 59.9 us (0.987)
  Pallas kernels: 20.3 us -> 22.2 us
  local copies, waits for them, and re-layouts: 2.44 us -> 0.65 us
  waiting for transfers between devices: 9.13 us -> 8.26 us
    unnamed x6 -> x2, local copies, waits for them, and re-layouts: 2.44 us -> 0.65 us
    ppermute x8, waiting for transfers between devices: 4.16 us -> 2.49 us  [from_offset(): lax.ppermute(value, axis, [((i + offset) % size, i) for i in range(size)])]
    pallas_call x1, Pallas kernels: 0.13 us -> 1.14 us  [local(): pl.pallas_call(prep_kernel, out_shape=pltpu.VMEM((NPT + 32 * F, NST), jnp...]
    pallas_call x1 -> x2, Pallas kernels: 2.1 us -> 2.97 us  [the longest x1 1.66 us: near_tile(): pl.pallas_call(near_kernel, in_specs=vmem(4), out_specs=ANY, scratch_shap...]
    all_to_all x1, waiting for transfers between devices: 1.66 us -> 2.46 us  [local(): shares = lax.all_to_all(partial.reshape(128, 4, NST), ALL, 0, 0, tiled=True)]
  transfers between devices with their start and end apart: 12 -> 12, of which waited for: 4 -> 4; matrix products, arithmetic and copies ran while one was open for 0% -> 0% of each run, Pallas kernels for 19% -> 21%
where the time goes in v3:
time: 59.9 us; the launch traced here: 59.5 us
  starting transfers between devices  27 us (45%)
  Pallas kernels  22.2 us (37%)
  waiting for transfers between devices  8.26 us (14%)
  between operations  0.75 us (1%)
  local copies, waits for them, and re-layouts  0.65 us (1%)
  other arithmetic  0.64 us (1%)
    ppermute x8, starting transfers between devices, from_offset(): lax.ppermute(value, axis, [((i + offset) % size, i) for i in range(size)])  21.4 us
    pallas_call x3, Pallas kernels, steer(): pl.pallas_call(steer_kernel, out_shape=pltpu.VMEM((F, 2, n, NPT, NST), jn...  9.43 us
    pallas_call x1, Pallas kernels, beams(): pl.pallas_call(beam_kernel, out_shape=pltpu.VMEM((F, 32, 4, NST), jnp.flo...  8.63 us
    all_to_all x1, starting transfers between devices, local(): shares = lax.all_to_all(partial.reshape(128, 4, NST), ALL, 0, 0, tiled=True)  4.88 us
    ppermute x3, waiting for transfers between devices, from_partner(): return lax.ppermute(value, 'win', [(i ^ bit, i) for i in range(4)])  3.31 us
    ppermute x8, waiting for transfers between devices, from_offset(): lax.ppermute(value, axis, [((i + offset) % size, i) for i in range(size)])  2.49 us
    all_to_all x1, waiting for transfers between devices, local(): shares = lax.all_to_all(partial.reshape(128, 4, NST), ALL, 0, 0, tiled=True)  2.46 us
    pallas_call x1, Pallas kernels, near_tile(): pl.pallas_call(near_kernel, in_specs=vmem(4), out_specs=ANY, scratch_shap...  1.66 us
  transfers between devices with their start and end apart: 12, of which 4 were waited for; matrix products, arithmetic and copies ran while one was open for 0% of the time, Pallas kernels for 21%

profile of v3, /device:TPU:0, one launch (start us, length us, event | category | flops | bytes accessed | tf_op | source)
XLA Modules:
  0.0 59.5 jit_solution(9933083785109502362)
XLA Ops:
  0.6 1.1 %prep.1.refs_0_ = s16[640,128]{1,0:T(8,128)(2,1)S(1)} custom-call(f32[4,2,16,128]{3,2,1,0:T(8,128)} %spectra_hbm.1, s32[128,512]{1,0:T(8,128)} %travel_hbm.1), custom_call_target="tpu_custom_call" | custom-call | tf_op jit(solution)/shard_map/prep/pallas_call | solution.py:300
  1.8 1.7 %collective-permute-start.2 = (s16[640,128]{1,0:T(8,128)(2,1)S(1)}, s16[640,128]{1,0:T(8,128)(2,1)S(1)}, u32[]{:S(2)}, u32[]{:S(2)}) collective-permute-start(s16[640,128]{1,0:T(8,128)(2,1)S(1)} %prep.1.refs_0_), channel_id=1, source_target_pairs={{24,0},{0,8},{8,16},{16,24},{25,1},{1,9},{9,17},{17,25},{26,2},{2,... | collective-permute-start | bytes 491528 | tf_op jit(solution)/shard_map/ppermute | solution.py:292
  3.5 2.7 %collective-permute-start.1 = (s16[640,128]{1,0:T(8,128)(2,1)S(1)}, s16[640,128]{1,0:T(8,128)(2,1)S(1)}, u32[]{:S(2)}, u32[]{:S(2)}) collective-permute-start(s16[640,128]{1,0:T(8,128)(2,1)S(1)} %prep.1.refs_0_), channel_id=1, source_target_pairs={{16,0},{24,8},{0,16},{8,24},{17,1},{25,9},{1,17},{9,25},{18,2},{26... | collective-permute-start | bytes 491528 | tf_op jit(solution)/shard_map/ppermute | solution.py:292
  6.2 3.9 %collective-permute-start.6 = (s16[640,128]{1,0:T(8,128)(2,1)S(1)}, s16[640,128]{1,0:T(8,128)(2,1)S(1)}, u32[]{:S(2)}, u32[]{:S(2)}) collective-permute-start(s16[640,128]{1,0:T(8,128)(2,1)S(1)} %prep.1.refs_0_), channel_id=1, source_target_pairs={{4,0},{5,1},{6,2},{7,3},{0,4},{1,5},{2,6},{3,7},{12,8},{13,9},{14,... | collective-permute-start | bytes 491528 | tf_op jit(solution)/shard_map/ppermute | solution.py:292
  10.1 1.4 %collective-permute-start = (s16[640,128]{1,0:T(8,128)(2,1)S(1)}, s16[640,128]{1,0:T(8,128)(2,1)S(1)}, u32[]{:S(2)}, u32[]{:S(2)}) collective-permute-start(s16[640,128]{1,0:T(8,128)(2,1)S(1)} %prep.1.refs_0_), channel_id=1, source_target_pairs={{8,0},{16,8},{24,16},{0,24},{9,1},{17,9},{25,17},{1,25},{10,2},{18... | collective-permute-start | bytes 491528 | tf_op jit(solution)/shard_map/ppermute | solution.py:292
  11.5 3.6 %collective-permute-start.5 = (s16[640,128]{1,0:T(8,128)(2,1)S(1)}, s16[640,128]{1,0:T(8,128)(2,1)S(1)}, u32[]{:S(2)}, u32[]{:S(2)}) collective-permute-start(s16[640,128]{1,0:T(8,128)(2,1)S(1)} %prep.1.refs_0_), channel_id=1, source_target_pairs={{5,0},{6,1},{7,2},{0,3},{1,4},{2,5},{3,6},{4,7},{13,8},{14,9},{15,... | collective-permute-start | bytes 491528 | tf_op jit(solution)/shard_map/ppermute | solution.py:292
  15.1 0.0 collective-permute-done.2.refs_2_.refs_3_
  15.1 2.2 %collective-permute-start.4 = (s16[640,128]{1,0:T(8,128)(2,1)S(1)}, s16[640,128]{1,0:T(8,128)(2,1)S(1)}, u32[]{:S(2)}, u32[]{:S(2)}) collective-permute-start(s16[640,128]{1,0:T(8,128)(2,1)S(1)} %prep.1.refs_0_), channel_id=1, source_target_pairs={{2,0},{3,1},{4,2},{5,3},{6,4},{7,5},{0,6},{1,7},{10,8},{11,9},{12,... | collective-permute-start | bytes 491528 | tf_op jit(solution)/shard_map/ppermute | solution.py:292
  17.4 2.9 %collective-permute-start.3 = (s16[640,128]{1,0:T(8,128)(2,1)S(1)}, s16[640,128]{1,0:T(8,128)(2,1)S(1)}, u32[]{:S(2)}, u32[]{:S(2)}) collective-permute-start(s16[640,128]{1,0:T(8,128)(2,1)S(1)} %prep.1.refs_0_), channel_id=1, source_target_pairs={{1,0},{2,1},{3,2},{4,3},{5,4},{6,5},{7,6},{0,7},{9,8},{10,9},{11,1... | collective-permute-start | bytes 491528 | tf_op jit(solution)/shard_map/ppermute | solution.py:292
  20.3 0.7 %copy-done = s32[4]{0:T(128)S(1)} copy-done((s32[4]{0:T(128)S(1)}, s32[4]{0:T(128)}, u32[]{:S(2)}) %copy-start) | copy-done | bytes 40
  20.9 1.5 %shard_map.50.own_steer = bf16[4,2,1,512,128]{4,3,2,1,0:T(8,128)(2,1)S(1)} custom-call(s32[4]{0:T(128)S(1)} %copy-done, s16[640,128]{1,0:T(8,128)(2,1)S(1)} %prep.1.refs_0_), custom_call_target="tpu_custom_call" | custom-call | tf_op jit(solution)/shard_map/pallas_call | solution.py:86
  22.5 3.5 %shard_map.51.row_steer = bf16[4,2,3,512,128]{4,3,2,1,0:T(8,128)(2,1)S(1)} custom-call(s32[4]{0:T(128)S(1)} %copy-done, s16[640,128]{1,0:T(8,128)(2,1)S(1)} %collective-permute-done.refs_0_.refs_1_, s16[640,128]{1,0:T(8,128)(2,1)S(1)} %collective-permute-done.1.refs_1_.refs_2_, s16[640,128]{1,0:T(8,128)(2,1)S(1)} %collective-permute-done.2.refs_2_.refs_3_), custom_call_target="tpu_custom_call" | custom-call | tf_op jit(solution)/shard_map/pallas_call | solution.py:86
  26.0 0.8 %collective-permute-start.7 = (s16[8,128,128]{2,1,0:T(8,128)(2,1)S(1)}, s16[8,128,128]{2,1,0:T(8,128)(2,1)S(1)}, u32[]{:S(2)}, u32[]{:S(2)}) collective-permute-start(s16[8,128,128]{2,1,0:T(8,128)(2,1)S(1)} %stack.1.a0), channel_id=1, source_target_pairs={{64,0},{96,32},{0,64},{32,96},{65,1},{97,33},{1,65},{33,97},{66,2}... | collective-permute-start | bytes 786440 | tf_op jit(solution)/shard_map/ppermute | solution.py:296
  26.8 4.4 %shard_map.52.col_steer = bf16[4,2,4,512,128]{4,3,2,1,0:T(8,128)(2,1)S(1)} custom-call(s32[4]{0:T(128)S(1)} %copy-done, s16[640,128]{1,0:T(8,128)(2,1)S(1)} %collective-permute-done.3.refs_4_.refs_0_, s16[640,128]{1,0:T(8,128)(2,1)S(1)} %collective-permute-done.4.refs_5_.refs_1_, s16[640,128]{1,0:T(8,128)(2,1)S(1)} %collective-permute-done.5.refs_6_.refs_2_, ...), custom_call_target="tpu_custom_call" | custom-call | tf_op jit(solution)/shard_map/pallas_call | solution.py:86
  31.2 1.8 %collective-permute-done.7.a1 = s16[8,128,128]{2,1,0:T(8,128)(2,1)S(1)} collective-permute-done((s16[8,128,128]{2,1,0:T(8,128)(2,1)S(1)}, s16[8,128,128]{2,1,0:T(8,128)(2,1)S(1)}, u32[]{:S(2)}, u32[]{:S(2)}) %collective-permute-start.7) | collective-permute-done | bytes 262176 | tf_op jit(solution)/shard_map/ppermute | solution.py:296
  33.0 1.5 %collective-permute-done.9.a3 = s16[8,128,128]{2,1,0:T(8,128)(2,1)S(1)} collective-permute-done((s16[8,128,128]{2,1,0:T(8,128)(2,1)S(1)}, s16[8,128,128]{2,1,0:T(8,128)(2,1)S(1)}, u32[]{:S(2)}, u32[]{:S(2)}) %collective-permute-start.9) | collective-permute-done | bytes 262176 | tf_op jit(solution)/shard_map/ppermute | solution.py:296
  34.5 8.6 %beams.1 = f32[4,32,4,128]{3,2,1,0:T(4,128)} custom-call(bf16[4,2,1,512,128]{4,3,2,1,0:T(8,128)(2,1)S(1)} %shard_map.50.own_steer, bf16[4,2,4,512,128]{4,3,2,1,0:T(8,128)(2,1)S(1)} %shard_map.52.col_steer, bf16[4,2,3,512,128]{4,3,2,1,0:T(8,128)(2,1)S(1)} %shard_map.51.row_steer, s16[8,128,128]{2,1,0:T(8,128)(2,1)S(1)} %stack.1.a0, ...), custom_call_target="tpu_custom_call" | custom-call | tf_op jit(solution)/shard_map/beams/pallas_call | solution.py:171
  43.2 4.9 %all-to-all-start = ((f32[128,4,128]{2,1,0:T(4,128)}), f32[128,4,128]{2,1,0:T(4,128)S(1)}, u32[]{:S(2)}, u32[]{:S(2)}) async-start(f32[128,4,128]{2,1,0:T(4,128)} %bitcast.1), calls=%async_computation | async-start | bytes 524288 | tf_op jit(solution)/shard_map/all_to_all | solution.py:328
  48.1 2.9 %collective-permute-start.10 = (s16[4,3,32,128]{3,2,1,0:T(8,128)(2,1)S(1)}, s16[4,3,32,128]{3,2,1,0:T(8,128)(2,1)S(1)}, u32[]{:S(2)}, u32[]{:S(2)}) collective-permute-start(s16[4,3,32,128]{3,2,1,0:T(8,128)(2,1)S(1)} %pack.1), channel_id=1, source_target_pairs={{2,0},{3,1},{4,2},{5,3},{6,4},{7,5},{0,6},{1,7},{10,8},{11,9},{12,... | collective-permute-start | bytes 294920 | tf_op jit(solution)/shard_map/ppermute | solution.py:292
  51.0 1.7 %near.1.old = bf16[2,4096,128]{2,1,0:T(8,128)(2,1)} custom-call(s16[8,128,128]{2,1,0:T(8,128)(2,1)S(1)} %stack.1.a0, s16[8,128,128]{2,1,0:T(8,128)(2,1)S(1)} %collective-permute-done.7.a1, s16[8,128,128]{2,1,0:T(8,128)(2,1)S(1)} %collective-permute-done.8.a2, s16[8,128,128]{2,1,0:T(8,128)(2,1)S(1)} %collective-permute-done.9.a3), custom_call_target="tpu_custom_call" | custom-call | tf_op jit(solution)/shard_map/near/pallas_call | solution.py:266
  52.7 2.5 %collective-permute-done.10.rows = s16[4,3,32,128]{3,2,1,0:T(8,128)(2,1)S(1)} collective-permute-done((s16[4,3,32,128]{3,2,1,0:T(8,128)(2,1)S(1)}, s16[4,3,32,128]{3,2,1,0:T(8,128)(2,1)S(1)}, u32[]{:S(2)}, u32[]{:S(2)}) %collective-permute-start.10) | collective-permute-done | bytes 98336 | tf_op jit(solution)/shard_map/ppermute | solution.py:292
  55.1 1.3 %far.1 = bf16[2,4096,128]{2,1,0:T(8,128)(2,1)} custom-call(s16[4,3,32,128]{3,2,1,0:T(8,128)(2,1)S(1)} %collective-permute-done.10.rows, s16[8,128,128]{2,1,0:T(8,128)(2,1)S(1)} %stack.1.a0, s16[8,128,128]{2,1,0:T(8,128)(2,1)S(1)} %collective-permute-done.7.a1, s16[8,128,128]{2,1,0:T(8,128)(2,1)S(1)} %collective-permute-done.8.a2, ...), custom_call_target="tpu_custom_call", output_to_operand_aliasing={{}: (5, {})} | custom-call | tf_op jit(solution)/shard_map/far/pallas_call | solution.py:278
  56.4 2.5 %all-to-all-done = f32[128,4,128]{2,1,0:T(4,128)S(1)} async-done(((f32[128,4,128]{2,1,0:T(4,128)}), f32[128,4,128]{2,1,0:T(4,128)S(1)}, u32[]{:S(2)}, u32[]{:S(2)}) %all-to-all-start) | async-done | bytes 262176 | tf_op jit(solution)/shard_map/all_to_all | solution.py:328
  58.9 0.6 %bitcast_reduce_fusion = f32[4,4,128]{2,1,0:T(4,128)} fusion(f32[128,4,128]{2,1,0:T(4,128)S(1)} %all-to-all-done), kind=kLoop, calls=%fused_computation | loop fusion | flops 63488 | bytes 270336 | tf_op jit(solution)/shard_map/reduce_sum | solution.py:330
  (12 shorter events, 0.1 us)
Async XLA Ops:
  1.8 13.4 %collective-permute-start.2 = (s16[640,128]{1,0:T(8,128)(2,1)S(1)}, s16[640,128]{1,0:T(8,128)(2,1)S(1)}, u32[]{:S(2)}, u32[]{:S(2)}) collective-permute-start(s16[640,128]{1,0:T(8,128)(2,1)S(1)} %prep.1.refs_0_), channel_id=1, source_target_pairs={{24,0},{0,8},{8,16},{16,24},{25,1},{1,9},{9,17},{17,25},{26,2},{2,... | collective-permute-start | bytes 491528 | tf_op jit(solution)/shard_map/ppermute | solution.py:292
  3.5 13.9 %collective-permute-start.1 = (s16[640,128]{1,0:T(8,128)(2,1)S(1)}, s16[640,128]{1,0:T(8,128)(2,1)S(1)}, u32[]{:S(2)}, u32[]{:S(2)}) collective-permute-start(s16[640,128]{1,0:T(8,128)(2,1)S(1)} %prep.1.refs_0_), channel_id=1, source_target_pairs={{16,0},{24,8},{0,16},{8,24},{17,1},{25,9},{1,17},{9,25},{18,2},{26... | collective-permute-start | bytes 491528 | tf_op jit(solution)/shard_map/ppermute | solution.py:292
  6.2 19.8 %collective-permute-start.6 = (s16[640,128]{1,0:T(8,128)(2,1)S(1)}, s16[640,128]{1,0:T(8,128)(2,1)S(1)}, u32[]{:S(2)}, u32[]{:S(2)}) collective-permute-start(s16[640,128]{1,0:T(8,128)(2,1)S(1)} %prep.1.refs_0_), channel_id=1, source_target_pairs={{4,0},{5,1},{6,2},{7,3},{0,4},{1,5},{2,6},{3,7},{12,8},{13,9},{14,... | collective-permute-start | bytes 491528 | tf_op jit(solution)/shard_map/ppermute | solution.py:292
  10.1 12.4 %collective-permute-start = (s16[640,128]{1,0:T(8,128)(2,1)S(1)}, s16[640,128]{1,0:T(8,128)(2,1)S(1)}, u32[]{:S(2)}, u32[]{:S(2)}) collective-permute-start(s16[640,128]{1,0:T(8,128)(2,1)S(1)} %prep.1.refs_0_), channel_id=1, source_target_pairs={{8,0},{16,8},{24,16},{0,24},{9,1},{17,9},{25,17},{1,25},{10,2},{18... | collective-permute-start | bytes 491528 | tf_op jit(solution)/shard_map/ppermute | solution.py:292
  11.5 14.5 %collective-permute-start.5 = (s16[640,128]{1,0:T(8,128)(2,1)S(1)}, s16[640,128]{1,0:T(8,128)(2,1)S(1)}, u32[]{:S(2)}, u32[]{:S(2)}) collective-permute-start(s16[640,128]{1,0:T(8,128)(2,1)S(1)} %prep.1.refs_0_), channel_id=1, source_target_pairs={{5,0},{6,1},{7,2},{0,3},{1,4},{2,5},{3,6},{4,7},{13,8},{14,9},{15,... | collective-permute-start | bytes 491528 | tf_op jit(solution)/shard_map/ppermute | solution.py:292
  15.1 10.8 %collective-permute-start.4 = (s16[640,128]{1,0:T(8,128)(2,1)S(1)}, s16[640,128]{1,0:T(8,128)(2,1)S(1)}, u32[]{:S(2)}, u32[]{:S(2)}) collective-permute-start(s16[640,128]{1,0:T(8,128)(2,1)S(1)} %prep.1.refs_0_), channel_id=1, source_target_pairs={{2,0},{3,1},{4,2},{5,3},{6,4},{7,5},{0,6},{1,7},{10,8},{11,9},{12,... | collective-permute-start | bytes 491528 | tf_op jit(solution)/shard_map/ppermute | solution.py:292
  17.4 8.6 %collective-permute-start.3 = (s16[640,128]{1,0:T(8,128)(2,1)S(1)}, s16[640,128]{1,0:T(8,128)(2,1)S(1)}, u32[]{:S(2)}, u32[]{:S(2)}) collective-permute-start(s16[640,128]{1,0:T(8,128)(2,1)S(1)} %prep.1.refs_0_), channel_id=1, source_target_pairs={{1,0},{2,1},{3,2},{4,3},{5,4},{6,5},{7,6},{0,7},{9,8},{10,9},{11,1... | collective-permute-start | bytes 491528 | tf_op jit(solution)/shard_map/ppermute | solution.py:292
  20.3 0.7 %copy-start = (s32[4]{0:T(128)S(1)}, s32[4]{0:T(128)}, u32[]{:S(2)}) copy-start(s32[4]{0:T(128)} %bins.5) | copy-start | bytes 52
  26.0 7.0 %collective-permute-start.7 = (s16[8,128,128]{2,1,0:T(8,128)(2,1)S(1)}, s16[8,128,128]{2,1,0:T(8,128)(2,1)S(1)}, u32[]{:S(2)}, u32[]{:S(2)}) collective-permute-start(s16[8,128,128]{2,1,0:T(8,128)(2,1)S(1)} %stack.1.a0), channel_id=1, source_target_pairs={{64,0},{96,32},{0,64},{32,96},{65,1},{97,33},{1,65},{33,97},{66,2}... | collective-permute-start | bytes 786440 | tf_op jit(solution)/shard_map/ppermute | solution.py:296
  26.8 6.2 %collective-permute-start.8 = (s16[8,128,128]{2,1,0:T(8,128)(2,1)S(1)}, s16[8,128,128]{2,1,0:T(8,128)(2,1)S(1)}, u32[]{:S(2)}, u32[]{:S(2)}) collective-permute-start(s16[8,128,128]{2,1,0:T(8,128)(2,1)S(1)} %stack.1.a0), channel_id=1, source_target_pairs={{32,0},{0,32},{96,64},{64,96},{33,1},{1,33},{97,65},{65,97},{34,2}... | collective-permute-start | bytes 786440 | tf_op jit(solution)/shard_map/ppermute | solution.py:296
  33.0 1.5 %collective-permute-start.9 = (s16[8,128,128]{2,1,0:T(8,128)(2,1)S(1)}, s16[8,128,128]{2,1,0:T(8,128)(2,1)S(1)}, u32[]{:S(2)}, u32[]{:S(2)}) collective-permute-start(s16[8,128,128]{2,1,0:T(8,128)(2,1)S(1)} %collective-permute-done.7.a1), channel_id=1, source_target_pairs={{32,0},{0,32},{96,64},{64,96},{33,1},{1,33},{97,65},{65,97},{34,2}... | collective-permute-start | bytes 786440 | tf_op jit(solution)/shard_map/ppermute | solution.py:296
  43.2 15.7 %all-to-all-start = ((f32[128,4,128]{2,1,0:T(4,128)}), f32[128,4,128]{2,1,0:T(4,128)S(1)}, u32[]{:S(2)}, u32[]{:S(2)}) async-start(f32[128,4,128]{2,1,0:T(4,128)} %bitcast.1), calls=%async_computation | async-start | bytes 524288 | tf_op jit(solution)/shard_map/all_to_all | solution.py:328
  48.1 7.0 %collective-permute-start.10 = (s16[4,3,32,128]{3,2,1,0:T(8,128)(2,1)S(1)}, s16[4,3,32,128]{3,2,1,0:T(8,128)(2,1)S(1)}, u32[]{:S(2)}, u32[]{:S(2)}) collective-permute-start(s16[4,3,32,128]{3,2,1,0:T(8,128)(2,1)S(1)} %pack.1), channel_id=1, source_target_pairs={{2,0},{3,1},{4,2},{5,3},{6,4},{7,5},{0,6},{1,7},{10,8},{11,9},{12,... | collective-permute-start | bytes 294920 | tf_op jit(solution)/shard_map/ppermute | solution.py:292

commit v4 on v3

--- a/solution.py
+++ b/solution.py
@@ -23,10 +23,11 @@
                             -1.331880156986464, 0.2196967900729894)]
 
 
-def prep_kernel(spectra_hbm, travel_hbm, payload, spectra, travel, sems):
+def prep_kernel(spectra_hbm, travel_hbm, bins_hbm, payload, scales, spectra, travel, bins, sems):
     moves = [
         pltpu.make_async_copy(spectra_hbm, spectra, sems.at[0]),
         pltpu.make_async_copy(travel_hbm, travel, sems.at[1]),
+        pltpu.make_async_copy(bins_hbm, bins, sems.at[2]),
     ]
     for move in moves:
         move.start()
@@ -42,6 +43,9 @@
             payload[at:at + 16, :] = value.astype(jnp.int32).astype(jnp.int16)
     moves[1].wait()
     payload[0:NPT, :] = travel[...].T.astype(jnp.int16)
+    moves[2].wait()
+    for f in range(F):
+        scales[f] = jnp.full((8, NST), bins[f].astype(jnp.float32) * (1.0 / NFFT), jnp.float32)
 
 
 def on_chip(*arrays):
@@ -56,7 +60,7 @@
 LIMIT = pltpu.CompilerParams(vmem_limit_bytes=16 * 2**20)
 
 
-def steer_kernel(bins, *refs):
+def steer_kernel(scales, *refs):
     payloads, out = refs[:-1], refs[-1]
     rows = 64
     for n, ref in enumerate(payloads):
@@ -64,8 +68,7 @@
             at = pl.ds(pl.multiple_of(i * rows, rows), rows)
             samples = (ref[at, :].astype(jnp.int32) & (NFFT - 1)).astype(jnp.float32)
             for f in range(F):
-                scale = bins[f].astype(jnp.float32) * (1.0 / NFFT)
-                turns = samples * scale
+                turns = (samples.reshape(rows // 8, 8, NST) * scales[f]).reshape(rows, NST)
                 r = turns - ((turns + ROUND) - ROUND)
                 z = r * r
                 s = SIN[4]
@@ -81,15 +84,15 @@
         lax.fori_loop(0, NPT // rows, chunk, 0)
 
 
-def steer(bins, payloads):
+def steer(scales, payloads):
     n = len(payloads)
     return pl.pallas_call(
         steer_kernel,
         out_shape=pltpu.VMEM((F, 2, n, NPT, NST), jnp.bfloat16),
-        in_specs=[SMEM] + vmem(n),
+        in_specs=vmem(n + 1),
         out_specs=vmem(1)[0],
         compiler_params=LIMIT,
-    )(pltpu.with_memory_space_constraint(bins, pltpu.SMEM), *on_chip(*payloads))
+    )(*on_chip(scales, *payloads))
 
 
 def stack_kernel(*refs):
@@ -109,7 +112,7 @@
 
 
 def decode(sources, block, f):
-    at = pl.ds(pl.multiple_of(32 * f, 32), 32)
+    at = slice(32 * f, 32 * f + 32) if isinstance(f, int) else pl.ds(pl.multiple_of(32 * f, 32), 32)
     return [
         (a[block, at, :].astype(jnp.int32).astype(jnp.float32) * (1.0 / 32768.0)).astype(jnp.bfloat16)
         for a in sources
@@ -159,18 +162,21 @@
             re, im = (own_steer[f, 0, 0], own_steer[f, 1, 0]) if k == 0 else (col_steer[f, 0, k - 1], col_steer[f, 1, k - 1])
             power = re.astype(jnp.float32) * image[:, :NST] + im.astype(jnp.float32) * image[:, NST:]
             total = power if total is None else total + power
+        values = []
         for j in range(4):
             value = jnp.sum(total[j * NST:(j + 1) * NST, :].T, axis=0, keepdims=True) * (1.0 / S)
-            beam[f, :, j, :] = jnp.broadcast_to(value, (32, NST))
+            values.append(value)
+        beam[f] = jnp.broadcast_to(jnp.concatenate(values, axis=0)[None], (32, 4, NST)).astype(jnp.bfloat16)
         return carry
 
-    lax.fori_loop(0, F, one, 0)
+    for f in range(F):
+        one(f, 0)
 
 
 def beams(own_steer, col_steer, row_steer, spectra):
     return pl.pallas_call(
         beam_kernel,
-        out_shape=pltpu.VMEM((F, 32, 4, NST), jnp.float32),
+        out_shape=pltpu.VMEM((F, 32, 4, NST), jnp.bfloat16),
         in_specs=vmem(7),
         out_specs=vmem(1)[0],
         scratch_shapes=[
@@ -297,28 +303,32 @@
 
 
 def local(spectra, bins, travel):
-    payload = pl.pallas_call(
+    payload, scales = pl.pallas_call(
         prep_kernel,
-        out_shape=pltpu.VMEM((NPT + 32 * F, NST), jnp.int16),
-        in_specs=[pl.BlockSpec(memory_space=pl.ANY)] * 2,
-        out_specs=vmem(1)[0],
+        out_shape=(
+            pltpu.VMEM((NPT + 32 * F, NST), jnp.int16),
+            pltpu.VMEM((F, 8, NST), jnp.float32),
+        ),
+        in_specs=[ANY] * 3,
+        out_specs=tuple(vmem(2)),
         scratch_shapes=[
             pltpu.VMEM(spectra.shape, jnp.float32),
             pltpu.VMEM(travel.shape, jnp.int32),
-            pltpu.SemaphoreType.DMA((2,)),
+            pltpu.SMEM((F,), jnp.int32),
+            pltpu.SemaphoreType.DMA((3,)),
         ],
         compiler_params=LIMIT,
         name="prep",
-    )(*(pltpu.with_memory_space_constraint(v, pltpu.HBM) for v in (spectra, travel)))
+    )(*(pltpu.with_memory_space_constraint(v, pltpu.HBM) for v in (spectra, travel, bins)))
     by_row = [from_offset(payload, "srow", d) for d in (1, 2, 3)]
     by_col = [from_offset(payload, "scol", d) for d in ROW_OFF[1:]]
-    steer0 = steer(bins, [payload])
-    steer2 = steer(bins, by_row)
+    steer0 = steer(scales, [payload])
+    steer2 = steer(scales, by_row)
     by_col, steer0, steer2 = lax.optimization_barrier((by_col, steer0, steer2))
     a0 = stack([payload] + by_row + by_col)
     a1 = from_partner(a0, 2)
     a2 = from_partner(a0, 1)
-    steer1 = steer(bins, by_col)
+    steer1 = steer(scales, by_col)
     a1, steer1 = lax.optimization_barrier((a1, steer1))
     a3 = from_partner(a1, 1)
     sources = (a0, a1, a2, a3)
@@ -327,7 +337,7 @@
     partial = beams(steer0, steer1, steer2, sources)
     shares = lax.all_to_all(partial.reshape(128, 4, NST), ALL, 0, 0, tiled=True)
     coherence = far_tile(rows, sources, near_tile(sources))
-    beam = shares.reshape(4, 32, 4, NST).sum(axis=1).reshape(1, 4 * NPT)
+    beam = shares.astype(jnp.float32).reshape(4, 32, 4, NST).sum(axis=1).reshape(1, 4 * NPT)
     return coherence.reshape(1, 2, 1024, 4, NST), beam
 
 

time: 59.9 us -> 57.7 us (0.963)
  Pallas kernels: 22.2 us -> 19.5 us
  starting transfers between devices: 27 us -> 28.7 us
  waiting for transfers between devices: 8.26 us -> 7.49 us
  local copies, waits for them, and re-layouts: 0.65 us -> 0 us
    all_to_all x1, starting transfers between devices: 4.88 us -> 6.57 us  [local(): shares = lax.all_to_all(partial.reshape(128, 4, NST), ALL, 0, 0, tiled=True)]
    pallas_call x3, Pallas kernels: 9.43 us -> 7.9 us  [steer(): pl.pallas_call(steer_kernel, out_shape=pltpu.VMEM((F, 2, n, NPT, NST), jn...]
    pallas_call x2, Pallas kernels: 9.77 us -> 8.62 us  [the longest x1 7.45 us: beams(): pl.pallas_call(beam_kernel, out_shape=pltpu.VMEM((F, 32, 4, NST), jnp.bfl...]
    ppermute x8, waiting for transfers between devices: 2.49 us -> 1.42 us  [from_offset(): lax.ppermute(value, axis, [((i + offset) % size, i) for i in range(size)])]
    unnamed x2 -> x0, local copies, waits for them, and re-layouts: 0.65 us -> none
  transfers between devices with their start and end apart: 12 -> 12, of which waited for: 4 -> 4; matrix products, arithmetic and copies ran while one was open for 0% -> 0% of each run, Pallas kernels for 21% -> 19%
where the time goes in v4:
time: 57.7 us; the launch traced here: 57.1 us
  starting transfers between devices  28.7 us (50%)
  Pallas kernels  19.5 us (34%)
  waiting for transfers between devices  7.49 us (13%)
  between operations  0.75 us (1%)
  other arithmetic  0.66 us (1%)
    ppermute x8, starting transfers between devices, from_offset(): lax.ppermute(value, axis, [((i + offset) % size, i) for i in range(size)])  21.4 us
    pallas_call x3, Pallas kernels, steer(): pl.pallas_call(steer_kernel, out_shape=pltpu.VMEM((F, 2, n, NPT, NST), jn...  7.9 us
    pallas_call x1, Pallas kernels, beams(): pl.pallas_call(beam_kernel, out_shape=pltpu.VMEM((F, 32, 4, NST), jnp.bfl...  7.45 us
    all_to_all x1, starting transfers between devices, local(): shares = lax.all_to_all(partial.reshape(128, 4, NST), ALL, 0, 0, tiled=True)  6.57 us
    ppermute x3, waiting for transfers between devices, from_partner(): return lax.ppermute(value, 'win', [(i ^ bit, i) for i in range(4)])  3.81 us
    all_to_all x1, waiting for transfers between devices, local(): shares = lax.all_to_all(partial.reshape(128, 4, NST), ALL, 0, 0, tiled=True)  2.26 us
    pallas_call x1, Pallas kernels, near_tile(): pl.pallas_call(near_kernel, in_specs=vmem(4), out_specs=ANY, scratch_shap...  1.67 us
    ppermute x8, waiting for transfers between devices, from_offset(): lax.ppermute(value, axis, [((i + offset) % size, i) for i in range(size)])  1.42 us
  transfers between devices with their start and end apart: 12, of which 4 were waited for; matrix products, arithmetic and copies ran while one was open for 0% of the time, Pallas kernels for 19%

profile of v4, /device:TPU:0, one launch (start us, length us, event | category | flops | bytes accessed | tf_op | source)
XLA Modules:
  0.0 57.1 jit_solution(11665200420659955812)
XLA Ops:
  0.6 1.2 %prep.1 = (s16[640,128]{1,0:T(8,128)(2,1)S(1)}, f32[4,8,128]{2,1,0:T(8,128)S(1)}) custom-call(f32[4,2,16,128]{3,2,1,0:T(8,128)} %spectra_hbm.1, s32[128,512]{1,0:T(8,128)} %travel_hbm.1, s32[4]{0:T(128)} %bins_hbm.1), custom_call_target="tpu_custom_call" | custom-call | tf_op jit(solution)/shard_map/prep/pallas_call | solution.py:306
  1.8 1.7 %collective-permute-start.2 = (s16[640,128]{1,0:T(8,128)(2,1)S(1)}, s16[640,128]{1,0:T(8,128)(2,1)S(1)}, u32[]{:S(2)}, u32[]{:S(2)}) collective-permute-start(s16[640,128]{1,0:T(8,128)(2,1)S(1)} %get-tuple-element.12.refs_0_), channel_id=1, source_target_pairs={{24,0},{0,8},{8,16},{16,24},{25,1},{1,9},{9,17},{17,25},{26,2},{2,... | collective-permute-start | bytes 491528 | tf_op jit(solution)/shard_map/ppermute | solution.py:298
  3.5 2.7 %collective-permute-start.1 = (s16[640,128]{1,0:T(8,128)(2,1)S(1)}, s16[640,128]{1,0:T(8,128)(2,1)S(1)}, u32[]{:S(2)}, u32[]{:S(2)}) collective-permute-start(s16[640,128]{1,0:T(8,128)(2,1)S(1)} %get-tuple-element.12.refs_0_), channel_id=1, source_target_pairs={{16,0},{24,8},{0,16},{8,24},{17,1},{25,9},{1,17},{9,25},{18,2},{26... | collective-permute-start | bytes 491528 | tf_op jit(solution)/shard_map/ppermute | solution.py:298
  6.2 3.9 %collective-permute-start.6 = (s16[640,128]{1,0:T(8,128)(2,1)S(1)}, s16[640,128]{1,0:T(8,128)(2,1)S(1)}, u32[]{:S(2)}, u32[]{:S(2)}) collective-permute-start(s16[640,128]{1,0:T(8,128)(2,1)S(1)} %get-tuple-element.12.refs_0_), channel_id=1, source_target_pairs={{4,0},{5,1},{6,2},{7,3},{0,4},{1,5},{2,6},{3,7},{12,8},{13,9},{14,... | collective-permute-start | bytes 491528 | tf_op jit(solution)/shard_map/ppermute | solution.py:298
  10.1 1.4 %collective-permute-start = (s16[640,128]{1,0:T(8,128)(2,1)S(1)}, s16[640,128]{1,0:T(8,128)(2,1)S(1)}, u32[]{:S(2)}, u32[]{:S(2)}) collective-permute-start(s16[640,128]{1,0:T(8,128)(2,1)S(1)} %get-tuple-element.12.refs_0_), channel_id=1, source_target_pairs={{8,0},{16,8},{24,16},{0,24},{9,1},{17,9},{25,17},{1,25},{10,2},{18... | collective-permute-start | bytes 491528 | tf_op jit(solution)/shard_map/ppermute | solution.py:298
  11.5 3.6 %collective-permute-start.5 = (s16[640,128]{1,0:T(8,128)(2,1)S(1)}, s16[640,128]{1,0:T(8,128)(2,1)S(1)}, u32[]{:S(2)}, u32[]{:S(2)}) collective-permute-start(s16[640,128]{1,0:T(8,128)(2,1)S(1)} %get-tuple-element.12.refs_0_), channel_id=1, source_target_pairs={{5,0},{6,1},{7,2},{0,3},{1,4},{2,5},{3,6},{4,7},{13,8},{14,9},{15,... | collective-permute-start | bytes 491528 | tf_op jit(solution)/shard_map/ppermute | solution.py:298
  15.2 2.2 %collective-permute-start.4 = (s16[640,128]{1,0:T(8,128)(2,1)S(1)}, s16[640,128]{1,0:T(8,128)(2,1)S(1)}, u32[]{:S(2)}, u32[]{:S(2)}) collective-permute-start(s16[640,128]{1,0:T(8,128)(2,1)S(1)} %get-tuple-element.12.refs_0_), channel_id=1, source_target_pairs={{2,0},{3,1},{4,2},{5,3},{6,4},{7,5},{0,6},{1,7},{10,8},{11,9},{12,... | collective-permute-start | bytes 491528 | tf_op jit(solution)/shard_map/ppermute | solution.py:298
  17.4 0.0 collective-permute-done.1.refs_1_.refs_2_
  17.4 2.9 %collective-permute-start.3 = (s16[640,128]{1,0:T(8,128)(2,1)S(1)}, s16[640,128]{1,0:T(8,128)(2,1)S(1)}, u32[]{:S(2)}, u32[]{:S(2)}) collective-permute-start(s16[640,128]{1,0:T(8,128)(2,1)S(1)} %get-tuple-element.12.refs_0_), channel_id=1, source_target_pairs={{1,0},{2,1},{3,2},{4,3},{5,4},{6,5},{7,6},{0,7},{9,8},{10,9},{11,1... | collective-permute-start | bytes 491528 | tf_op jit(solution)/shard_map/ppermute | solution.py:298
  20.3 1.0 %shard_map.50.own_steer = bf16[4,2,1,512,128]{4,3,2,1,0:T(8,128)(2,1)S(1)} custom-call(f32[4,8,128]{2,1,0:T(8,128)S(1)} %get-tuple-element.13.scales, s16[640,128]{1,0:T(8,128)(2,1)S(1)} %get-tuple-element.12.refs_0_), custom_call_target="tpu_custom_call" | custom-call | tf_op jit(solution)/shard_map/pallas_call | solution.py:89
  21.3 3.0 %shard_map.51.row_steer = bf16[4,2,3,512,128]{4,3,2,1,0:T(8,128)(2,1)S(1)} custom-call(f32[4,8,128]{2,1,0:T(8,128)S(1)} %get-tuple-element.13.scales, s16[640,128]{1,0:T(8,128)(2,1)S(1)} %collective-permute-done.refs_0_.refs_1_, s16[640,128]{1,0:T(8,128)(2,1)S(1)} %collective-permute-done.1.refs_1_.refs_2_, ...), custom_call_target="tpu_custom_call" | custom-call | tf_op jit(solution)/shard_map/pallas_call | solution.py:89
  24.3 0.0 collective-permute-done.6.refs_7_.refs_3_
  24.3 0.8 %collective-permute-start.7 = (s16[8,128,128]{2,1,0:T(8,128)(2,1)S(1)}, s16[8,128,128]{2,1,0:T(8,128)(2,1)S(1)}, u32[]{:S(2)}, u32[]{:S(2)}) collective-permute-start(s16[8,128,128]{2,1,0:T(8,128)(2,1)S(1)} %stack.1.a0), channel_id=1, source_target_pairs={{64,0},{96,32},{0,64},{32,96},{65,1},{97,33},{1,65},{33,97},{66,2}... | collective-permute-start | bytes 786440 | tf_op jit(solution)/shard_map/ppermute | solution.py:302
  25.1 3.9 %shard_map.52.col_steer = bf16[4,2,4,512,128]{4,3,2,1,0:T(8,128)(2,1)S(1)} custom-call(f32[4,8,128]{2,1,0:T(8,128)S(1)} %get-tuple-element.13.scales, s16[640,128]{1,0:T(8,128)(2,1)S(1)} %collective-permute-done.3.refs_4_.refs_0_, s16[640,128]{1,0:T(8,128)(2,1)S(1)} %collective-permute-done.4.refs_5_.refs_1_, ...), custom_call_target="tpu_custom_call" | custom-call | tf_op jit(solution)/shard_map/pallas_call | solution.py:89
  29.1 2.3 %collective-permute-done.7.a1 = s16[8,128,128]{2,1,0:T(8,128)(2,1)S(1)} collective-permute-done((s16[8,128,128]{2,1,0:T(8,128)(2,1)S(1)}, s16[8,128,128]{2,1,0:T(8,128)(2,1)S(1)}, u32[]{:S(2)}, u32[]{:S(2)}) %collective-permute-start.7) | collective-permute-done | bytes 262176 | tf_op jit(solution)/shard_map/ppermute | solution.py:302
  31.3 1.5 %collective-permute-done.9.a3 = s16[8,128,128]{2,1,0:T(8,128)(2,1)S(1)} collective-permute-done((s16[8,128,128]{2,1,0:T(8,128)(2,1)S(1)}, s16[8,128,128]{2,1,0:T(8,128)(2,1)S(1)}, u32[]{:S(2)}, u32[]{:S(2)}) %collective-permute-start.9) | collective-permute-done | bytes 262176 | tf_op jit(solution)/shard_map/ppermute | solution.py:302
  32.9 7.5 %beams.1 = bf16[4,32,4,128]{3,2,1,0:T(4,128)(2,1)} custom-call(bf16[4,2,1,512,128]{4,3,2,1,0:T(8,128)(2,1)S(1)} %shard_map.50.own_steer, bf16[4,2,4,512,128]{4,3,2,1,0:T(8,128)(2,1)S(1)} %shard_map.52.col_steer, bf16[4,2,3,512,128]{4,3,2,1,0:T(8,128)(2,1)S(1)} %shard_map.51.row_steer, s16[8,128,128]{2,1,0:T(8,128)(2,1)S(1)} %stack.1.a0, ...), custom_call_target="tpu_custom_call" | custom-call | tf_op jit(solution)/shard_map/beams/pallas_call | solution.py:177
  40.3 6.6 %all-to-all-start = ((bf16[128,4,128]{2,1,0:T(4,128)(2,1)}), bf16[128,4,128]{2,1,0:T(4,128)(2,1)S(1)}, u32[]{:S(2)}, u32[]{:S(2)}) async-start(bf16[128,4,128]{2,1,0:T(4,128)(2,1)} %bitcast.1), calls=%async_computation | async-start | bytes 262144 | tf_op jit(solution)/shard_map/all_to_all | solution.py:338
  46.9 2.9 %collective-permute-start.10 = (s16[4,3,32,128]{3,2,1,0:T(8,128)(2,1)S(1)}, s16[4,3,32,128]{3,2,1,0:T(8,128)(2,1)S(1)}, u32[]{:S(2)}, u32[]{:S(2)}) collective-permute-start(s16[4,3,32,128]{3,2,1,0:T(8,128)(2,1)S(1)} %pack.1), channel_id=1, source_target_pairs={{2,0},{3,1},{4,2},{5,3},{6,4},{7,5},{0,6},{1,7},{10,8},{11,9},{12,... | collective-permute-start | bytes 294920 | tf_op jit(solution)/shard_map/ppermute | solution.py:298
  49.8 1.7 %near.1.old = bf16[2,4096,128]{2,1,0:T(8,128)(2,1)} custom-call(s16[8,128,128]{2,1,0:T(8,128)(2,1)S(1)} %stack.1.a0, s16[8,128,128]{2,1,0:T(8,128)(2,1)S(1)} %collective-permute-done.7.a1, s16[8,128,128]{2,1,0:T(8,128)(2,1)S(1)} %collective-permute-done.8.a2, s16[8,128,128]{2,1,0:T(8,128)(2,1)S(1)} %collective-permute-done.9.a3), custom_call_target="tpu_custom_call" | custom-call | tf_op jit(solution)/shard_map/near/pallas_call | solution.py:272
  51.5 1.4 %collective-permute-done.10.rows = s16[4,3,32,128]{3,2,1,0:T(8,128)(2,1)S(1)} collective-permute-done((s16[4,3,32,128]{3,2,1,0:T(8,128)(2,1)S(1)}, s16[4,3,32,128]{3,2,1,0:T(8,128)(2,1)S(1)}, u32[]{:S(2)}, u32[]{:S(2)}) %collective-permute-start.10) | collective-permute-done | bytes 98336 | tf_op jit(solution)/shard_map/ppermute | solution.py:298
  52.9 1.3 %far.1 = bf16[2,4096,128]{2,1,0:T(8,128)(2,1)} custom-call(s16[4,3,32,128]{3,2,1,0:T(8,128)(2,1)S(1)} %collective-permute-done.10.rows, s16[8,128,128]{2,1,0:T(8,128)(2,1)S(1)} %stack.1.a0, s16[8,128,128]{2,1,0:T(8,128)(2,1)S(1)} %collective-permute-done.7.a1, s16[8,128,128]{2,1,0:T(8,128)(2,1)S(1)} %collective-permute-done.8.a2, ...), custom_call_target="tpu_custom_call", output_to_operand_aliasing={{}: (5, {})} | custom-call | tf_op jit(solution)/shard_map/far/pallas_call | solution.py:284
  54.2 2.3 %all-to-all-done = bf16[128,4,128]{2,1,0:T(4,128)(2,1)S(1)} async-done(((bf16[128,4,128]{2,1,0:T(4,128)(2,1)}), bf16[128,4,128]{2,1,0:T(4,128)(2,1)S(1)}, u32[]{:S(2)}, u32[]{:S(2)}) %all-to-all-start) | async-done | bytes 131104 | tf_op jit(solution)/shard_map/all_to_all | solution.py:338
  56.5 0.7 %convert_reduce_fusion = f32[4,4,128]{2,1,0:T(4,128)} fusion(bf16[128,4,128]{2,1,0:T(4,128)(2,1)S(1)} %all-to-all-done), kind=kLoop, calls=%fused_computation | loop fusion | flops 129024 | bytes 139264 | tf_op jit(solution)/shard_map/reduce_sum | solution.py:340
  (10 shorter events, 0.1 us)
Async XLA Ops:
  1.8 13.4 %collective-permute-start.2 = (s16[640,128]{1,0:T(8,128)(2,1)S(1)}, s16[640,128]{1,0:T(8,128)(2,1)S(1)}, u32[]{:S(2)}, u32[]{:S(2)}) collective-permute-start(s16[640,128]{1,0:T(8,128)(2,1)S(1)} %get-tuple-element.12.refs_0_), channel_id=1, source_target_pairs={{24,0},{0,8},{8,16},{16,24},{25,1},{1,9},{9,17},{17,25},{26,2},{2,... | collective-permute-start | bytes 491528 | tf_op jit(solution)/shard_map/ppermute | solution.py:298
  3.5 13.9 %collective-permute-start.1 = (s16[640,128]{1,0:T(8,128)(2,1)S(1)}, s16[640,128]{1,0:T(8,128)(2,1)S(1)}, u32[]{:S(2)}, u32[]{:S(2)}) collective-permute-start(s16[640,128]{1,0:T(8,128)(2,1)S(1)} %get-tuple-element.12.refs_0_), channel_id=1, source_target_pairs={{16,0},{24,8},{0,16},{8,24},{17,1},{25,9},{1,17},{9,25},{18,2},{26... | collective-permute-start | bytes 491528 | tf_op jit(solution)/shard_map/ppermute | solution.py:298
  6.2 18.1 %collective-permute-start.6 = (s16[640,128]{1,0:T(8,128)(2,1)S(1)}, s16[640,128]{1,0:T(8,128)(2,1)S(1)}, u32[]{:S(2)}, u32[]{:S(2)}) collective-permute-start(s16[640,128]{1,0:T(8,128)(2,1)S(1)} %get-tuple-element.12.refs_0_), channel_id=1, source_target_pairs={{4,0},{5,1},{6,2},{7,3},{0,4},{1,5},{2,6},{3,7},{12,8},{13,9},{14,... | collective-permute-start | bytes 491528 | tf_op jit(solution)/shard_map/ppermute | solution.py:298
  10.1 11.2 %collective-permute-start = (s16[640,128]{1,0:T(8,128)(2,1)S(1)}, s16[640,128]{1,0:T(8,128)(2,1)S(1)}, u32[]{:S(2)}, u32[]{:S(2)}) collective-permute-start(s16[640,128]{1,0:T(8,128)(2,1)S(1)} %get-tuple-element.12.refs_0_), channel_id=1, source_target_pairs={{8,0},{16,8},{24,16},{0,24},{9,1},{17,9},{25,17},{1,25},{10,2},{18... | collective-permute-start | bytes 491528 | tf_op jit(solution)/shard_map/ppermute | solution.py:298
  11.5 12.8 %collective-permute-start.5 = (s16[640,128]{1,0:T(8,128)(2,1)S(1)}, s16[640,128]{1,0:T(8,128)(2,1)S(1)}, u32[]{:S(2)}, u32[]{:S(2)}) collective-permute-start(s16[640,128]{1,0:T(8,128)(2,1)S(1)} %get-tuple-element.12.refs_0_), channel_id=1, source_target_pairs={{5,0},{6,1},{7,2},{0,3},{1,4},{2,5},{3,6},{4,7},{13,8},{14,9},{15,... | collective-permute-start | bytes 491528 | tf_op jit(solution)/shard_map/ppermute | solution.py:298
  15.2 9.1 %collective-permute-start.4 = (s16[640,128]{1,0:T(8,128)(2,1)S(1)}, s16[640,128]{1,0:T(8,128)(2,1)S(1)}, u32[]{:S(2)}, u32[]{:S(2)}) collective-permute-start(s16[640,128]{1,0:T(8,128)(2,1)S(1)} %get-tuple-element.12.refs_0_), channel_id=1, source_target_pairs={{2,0},{3,1},{4,2},{5,3},{6,4},{7,5},{0,6},{1,7},{10,8},{11,9},{12,... | collective-permute-start | bytes 491528 | tf_op jit(solution)/shard_map/ppermute | solution.py:298
  17.4 6.9 %collective-permute-start.3 = (s16[640,128]{1,0:T(8,128)(2,1)S(1)}, s16[640,128]{1,0:T(8,128)(2,1)S(1)}, u32[]{:S(2)}, u32[]{:S(2)}) collective-permute-start(s16[640,128]{1,0:T(8,128)(2,1)S(1)} %get-tuple-element.12.refs_0_), channel_id=1, source_target_pairs={{1,0},{2,1},{3,2},{4,3},{5,4},{6,5},{7,6},{0,7},{9,8},{10,9},{11,1... | collective-permute-start | bytes 491528 | tf_op jit(solution)/shard_map/ppermute | solution.py:298
  24.3 7.0 %collective-permute-start.7 = (s16[8,128,128]{2,1,0:T(8,128)(2,1)S(1)}, s16[8,128,128]{2,1,0:T(8,128)(2,1)S(1)}, u32[]{:S(2)}, u32[]{:S(2)}) collective-permute-start(s16[8,128,128]{2,1,0:T(8,128)(2,1)S(1)} %stack.1.a0), channel_id=1, source_target_pairs={{64,0},{96,32},{0,64},{32,96},{65,1},{97,33},{1,65},{33,97},{66,2}... | collective-permute-start | bytes 786440 | tf_op jit(solution)/shard_map/ppermute | solution.py:302
  25.1 6.2 %collective-permute-start.8 = (s16[8,128,128]{2,1,0:T(8,128)(2,1)S(1)}, s16[8,128,128]{2,1,0:T(8,128)(2,1)S(1)}, u32[]{:S(2)}, u32[]{:S(2)}) collective-permute-start(s16[8,128,128]{2,1,0:T(8,128)(2,1)S(1)} %stack.1.a0), channel_id=1, source_target_pairs={{32,0},{0,32},{96,64},{64,96},{33,1},{1,33},{97,65},{65,97},{34,2}... | collective-permute-start | bytes 786440 | tf_op jit(solution)/shard_map/ppermute | solution.py:302
  31.3 1.5 %collective-permute-start.9 = (s16[8,128,128]{2,1,0:T(8,128)(2,1)S(1)}, s16[8,128,128]{2,1,0:T(8,128)(2,1)S(1)}, u32[]{:S(2)}, u32[]{:S(2)}) collective-permute-start(s16[8,128,128]{2,1,0:T(8,128)(2,1)S(1)} %collective-permute-done.7.a1), channel_id=1, source_target_pairs={{32,0},{0,32},{96,64},{64,96},{33,1},{1,33},{97,65},{65,97},{34,2}... | collective-permute-start | bytes 786440 | tf_op jit(solution)/shard_map/ppermute | solution.py:302
  40.3 16.2 %all-to-all-start = ((bf16[128,4,128]{2,1,0:T(4,128)(2,1)}), bf16[128,4,128]{2,1,0:T(4,128)(2,1)S(1)}, u32[]{:S(2)}, u32[]{:S(2)}) async-start(bf16[128,4,128]{2,1,0:T(4,128)(2,1)} %bitcast.1), calls=%async_computation | async-start | bytes 262144 | tf_op jit(solution)/shard_map/all_to_all | solution.py:338
  46.9 6.0 %collective-permute-start.10 = (s16[4,3,32,128]{3,2,1,0:T(8,128)(2,1)S(1)}, s16[4,3,32,128]{3,2,1,0:T(8,128)(2,1)S(1)}, u32[]{:S(2)}, u32[]{:S(2)}) collective-permute-start(s16[4,3,32,128]{3,2,1,0:T(8,128)(2,1)S(1)} %pack.1), channel_id=1, source_target_pairs={{2,0},{3,1},{4,2},{5,3},{6,4},{7,5},{0,6},{1,7},{10,8},{11,9},{12,... | collective-permute-start | bytes 294920 | tf_op jit(solution)/shard_map/ppermute | solution.py:298
